TPU v7x, 128 devices: a whole 4x4x4 slice. The times are simulated.
128 devices in a mesh: req: 64 (over y, x, z), head: 2 (over core).
Axes of the slice: x: 4, y: 4, z: 4, core: 2. Of those that a mesh axis runs over, the one named last changes fastest.
Arguments:
- hidden_in: bfloat16 [4096, 2048], P('req'), may hold values from -14 to 14
- attn_gain: float32 [2048], replicated, may hold values from 0.1 to 1.9
- w_query: bfloat16 [2048, 2048], P(None, 'head'), may hold values from -0.125 to 0.125
- w_key: bfloat16 [2048, 1024], P(None, 'head'), may hold values from -0.125 to 0.125
- w_value: bfloat16 [2048, 1024], P(None, 'head'), may hold values from -0.125 to 0.125
- query_gain: float32 [128], replicated, may hold values from 0.5 to 2
- key_gain: float32 [128], replicated, may hold values from 0.5 to 2
- w_out: bfloat16 [2048, 2048], P('head'), may hold values from -0.125 to 0.125
- cache_keys: bfloat16 [64, 2048, 1024], P('req', None, 'head'), may hold values from -3.5 to 3.5
- cache_values: bfloat16 [64, 2048, 1024], P('req', None, 'head'), may hold values from -6 to 6
- cache_lengths: int32 [64], replicated, may hold values from 1 to 2048, 65536 in all
- slot_request: int32 [64], replicated, may hold values from 0 to 63, each once
- mlp_gain: float32 [2048], P('head'), may hold values from 0.1 to 1.9
- w_gate: bfloat16 [2048, 6144], P('head', 'req'), may hold values from -0.125 to 0.125
- w_up: bfloat16 [2048, 6144], P('head', 'req'), may hold values from -0.125 to 0.125
- w_down: bfloat16 [6144, 2048], P('req', 'head'), may hold values from -0.078125 to 0.078125
- final_gain: float32 [2048], replicated, may hold values from 0.1 to 1.9
- w_vocab: bfloat16 [2048, 151936], P(None, ('req', 'head')), may hold values from -8 to 8
Outputs:
- hidden_out: bfloat16 [4096, 2048], P('req', 'head')
- log_probs: float32 [64, 151936], P(None, ('req', 'head'))
Inputs may be any that keep to these rules, and one draw needn't show every extreme that they name: `cache_lengths`: the largest length is exactly 2048. `slot_request`: each request appears once.
All inputs are finite; a program needn't handle non-finite values.
Results may differ from a plain program's by a relative error of at most 0.008.
Values may be sent and summed in bfloat16 or wider, within the bound.
A program may use at most 128 MiB of HBM per device.

v0:
```python
import jax
import jax.numpy as jnp
from jax import lax
from jax.sharding import PartitionSpec as P

D = 2048
HEAD_DIM = 128


EPS = 1e-06
ROPE_BASE = 1000000.0
NEG = -1e30


def norm_rows(field, gain_vec):
    return field * lax.rsqrt(jnp.mean(field * field, axis=-1, keepdims=True) + EPS) * gain_vec


def rotate(field, positions):
    half_dim = field.shape[-1] // 2
    frequency = ROPE_BASE ** (-2.0 * jnp.arange(half_dim, dtype=jnp.float32) / field.shape[-1])
    angles = positions[..., None, None] * frequency
    cosine = jnp.cos(angles)
    sines = jnp.sin(angles)
    lower_half = field[..., :half_dim]
    upper_half = field[..., half_dim:]
    return jnp.concatenate(
        [lower_half * cosine - upper_half * sines, upper_half * cosine + lower_half * sines],
        axis=-1,
    )


def inverse_order(slot_request):
    indices = jnp.arange(slot_request.shape[0], dtype=jnp.int32)
    return jnp.sum(
        jnp.where(slot_request[None, :] == indices[:, None], indices[None, :], 0), axis=1
    )


def attend_slot(queries, keys_new, values_new, keys_cache, values_cache, cache_len):
    row_count, value_heads, head_size = keys_new.shape
    group_size = queries.shape[1] // value_heads
    grouped = queries.reshape(row_count, value_heads, group_size, head_size)
    score_scale = head_size ** (-0.5)
    recent = (
        jnp.einsum("skgd,tkd->kgst", grouped, keys_new, preferred_element_type=jnp.float32)
        * score_scale
    )
    causal = jnp.arange(row_count)[:, None] >= jnp.arange(row_count)[None, :]
    recent = jnp.where(causal, recent, NEG)
    cache_span = keys_cache.shape[0]
    stored = (
        jnp.einsum("skgd,lkd->kgsl", grouped, keys_cache, preferred_element_type=jnp.float32)
        * score_scale
    )
    stored = jnp.where(jnp.arange(cache_span, dtype=jnp.int32) < cache_len, stored, NEG)
    old_weights = jnp.exp(stored)
    new_weights = jnp.exp(recent)
    row_total = jnp.sum(old_weights, axis=-1) + jnp.sum(new_weights, axis=-1)
    old_weights = (old_weights / row_total[..., None]).astype(jnp.bfloat16)
    new_weights = (new_weights / row_total[..., None]).astype(jnp.bfloat16)
    blended = jnp.einsum(
        "kgsl,lkd->skgd", old_weights, values_cache, preferred_element_type=jnp.float32
    )
    blended = blended + jnp.einsum(
        "kgst,tkd->skgd", new_weights, values_new, preferred_element_type=jnp.float32
    )
    return blended.reshape(row_count, value_heads * group_size * head_size).astype(jnp.bfloat16)


def on_device(
    hidden_in,
    attn_gain,
    w_query,
    w_key,
    w_value,
    query_gain,
    key_gain,
    w_out,
    cache_keys,
    cache_values,
    cache_lengths,
    slot_request,
    mlp_gain,
    w_gate,
    w_up,
    w_down,
    final_gain,
    w_vocab,
):
    row_count = hidden_in.shape[0]
    half_width = mlp_gain.shape[0]
    slot_index = lax.axis_index("req")
    request_id = lax.dynamic_index_in_dim(slot_request, slot_index, 0, keepdims=False)
    cache_len = lax.dynamic_index_in_dim(cache_lengths, request_id, 0, keepdims=False)
    tokens = hidden_in.astype(jnp.float32)
    normed = norm_rows(tokens, attn_gain).astype(jnp.bfloat16)
    query_heads = w_query.shape[1] // HEAD_DIM
    value_heads = w_key.shape[1] // HEAD_DIM
    positions = (cache_len + jnp.arange(row_count, dtype=jnp.int32)).astype(jnp.float32)
    queries = jnp.dot(normed, w_query, preferred_element_type=jnp.float32).reshape(
        row_count, query_heads, HEAD_DIM
    )
    queries = rotate(norm_rows(queries, query_gain), positions).astype(jnp.bfloat16)
    keys_new = jnp.dot(normed, w_key, preferred_element_type=jnp.float32).reshape(
        row_count, value_heads, HEAD_DIM
    )
    keys_new = rotate(norm_rows(keys_new, key_gain), positions).astype(jnp.bfloat16)
    values_new = (
        jnp.dot(normed, w_value, preferred_element_type=jnp.float32)
        .astype(jnp.bfloat16)
        .reshape(row_count, value_heads, HEAD_DIM)
    )
    keys_cache = cache_keys.reshape(cache_keys.shape[1], value_heads, HEAD_DIM)
    values_cache = cache_values.reshape(cache_values.shape[1], value_heads, HEAD_DIM)
    attended = attend_slot(queries, keys_new, values_new, keys_cache, values_cache, cache_len)
    projected = jnp.dot(attended, w_out, preferred_element_type=jnp.float32)
    own_sum = lax.psum_scatter(
        projected.astype(jnp.bfloat16), "head", scatter_dimension=1, tiled=True
    ).astype(jnp.float32)
    head_part = lax.axis_index("head")
    residual = lax.dynamic_slice_in_dim(tokens, head_part * half_width, half_width, 1) + own_sum
    squares = lax.psum(jnp.sum(residual * residual, axis=1), "head")
    mixed_rows = (residual * lax.rsqrt(squares[:, None] / D + EPS) * mlp_gain).astype(jnp.bfloat16)
    paired = jnp.concatenate([w_gate, w_up], axis=1)
    partial_rows = jnp.dot(
        lax.all_gather(mixed_rows, "req", axis=0, tiled=True),
        paired,
        preferred_element_type=jnp.float32,
    )
    summed_rows = lax.psum(partial_rows.astype(jnp.bfloat16), "head").astype(jnp.float32)
    unit_count = w_gate.shape[1]
    active = (jax.nn.silu(summed_rows[:, :unit_count]) * summed_rows[:, unit_count:]).astype(
        jnp.bfloat16
    )
    down_part = lax.psum_scatter(
        jnp.dot(active, w_down, preferred_element_type=jnp.float32),
        "req",
        scatter_dimension=0,
        tiled=True,
    )
    output = residual + down_part
    hidden_out = output.astype(jnp.bfloat16)
    last_row = output[row_count - 1 :, :]
    collected = lax.all_gather(last_row, ("req", "head"), axis=1, tiled=True).reshape(-1, D)
    final_rows = norm_rows(collected, final_gain).astype(jnp.bfloat16)
    logits = jnp.dot(final_rows, w_vocab, preferred_element_type=jnp.float32)
    row_max = lax.pmax(jnp.max(logits, axis=1), ("req", "head"))
    row_total = lax.psum(jnp.sum(jnp.exp(logits - row_max[:, None]), axis=1), ("req", "head"))
    log_probs = logits - row_max[:, None] - jnp.log(row_total)[:, None]
    log_probs = jnp.take(log_probs, inverse_order(slot_request), axis=0)
    return (hidden_out, log_probs)


def solution(mesh):
    in_specs = (
        P("req", None),
        P(),
        P(None, "head"),
        P(None, "head"),
        P(None, "head"),
        P(),
        P(),
        P("head", None),
        P("req", None, "head"),
        P("req", None, "head"),
        P(),
        P(),
        P("head"),
        P("head", "req"),
        P("head", "req"),
        P("req", "head"),
        P(),
        P(None, ("req", "head")),
    )
    out_specs = (P("req", "head"), P(None, ("req", "head")))
    return jax.shard_map(
        on_device, mesh=mesh, in_specs=in_specs, out_specs=out_specs, check_vma=False
    )
```

profile of v0, /device:TPU:1, one launch (start us, length us, event | category | flops | bytes accessed | tf_op | source)
XLA Modules:
  0.0 747.4 jit_solution(8484590395757010456)
XLA Ops:
  7.2 1.4 dynamic_slice.11
  10.6 1.2 dynamic_slice.12
  11.8 0.6 add_convert_fusion.2
  12.5 0.7 iota_compare_fusion.2
  13.2 1.1 multiply_reduce_fusion.1
  14.3 3.2 convolution_bitcast_fusion
  17.5 0.1 multiply_reduce_fusion.3
  17.8 0.1 copy.64
  17.9 0.2 multiply_cosine_fusion
  18.1 0.1 multiply_multiply_fusion
  18.2 0.2 subtract_convert_fusion
  18.5 4.0 reshape.165
  22.5 0.5 fusion.40
  23.0 0.1 multiply_reduce_fusion.4
  23.3 0.1 fusion.27
  23.4 0.1 subtract_convert_fusion.1
  23.5 4.1 reshape.167
  27.6 0.5 convolution_convert_fusion.2
  28.1 3.2 bitcast_reduce_fusion
  31.4 0.3 fusion.43
  31.8 1.4 fusion.12
  33.2 0.2 fusion.17
  33.4 0.1 copy.73
  33.7 3.8 convolution_convert_fusion.1
  37.6 14.1 %reduce-scatter.3.cloned.1.call-done = bf16[64,1024]{1,0:T(8,128)(2,1)} async-done(((bf16[64,2048]{1,0:T(8,128)(2,1)}), bf16[64,1024]{1,0:T(8,128)(2,1)}) %reduce-scatter.3.cloned.1.call-update) | async-done | bytes 131088 | tf_op jit(solution)/shard_map/reduce_scatter | solution.py:118
  51.6 1.0 multiply_reduce_fusion.2
  52.7 2.5 psum.21
  55.2 1.7 multiply_convert_fusion.3
  56.9 79.7 %all-gather.2.cloned.1.call-done = bf16[4096,1024]{1,0:T(8,128)(2,1)} async-done(((bf16[64,1024]{1,0:T(8,128)(2,1)}), bf16[4096,1024]{1,0:T(8,128)(2,1)}) %all-gather.2.cloned.1.call-update) | async-done | bytes 8388624 | tf_op jit(solution)/shard_map/all_gather | solution.py:127
  136.6 7.5 %convolution_convert_fusion = bf16[4096,192]{0,1:T(8,128)(2,1)} fusion(bf16[4096,1024]{1,0:T(8,128)(2,1)} %all-gather.2.cloned.1.call-done, bf16[1024,96]{0,1:T(8,128)(2,1)S(1)} %copy-done.12, bf16[1024,96]{0,1:T(8,128)(2,1)S(1)} %copy-done.13), kind=kOutput, calls=%fused_computation.1 | convolution fusion | flops 1612185600 | bytes 10354688 | tf_op jit(solution)/shard_map/dot_general | solution.py:126
  144.2 26.1 %all-reduce.2.cloned.1.call-done = bf16[4096,192]{0,1:T(8,128)(2,1)} async-done(((bf16[4096,192]{0,1:T(8,128)(2,1)}), bf16[4096,192]{0,1:T(8,128)(2,1)}) %all-reduce.2.cloned.1.call-update) | async-done | bytes 1572880 | tf_op jit(solution)/shard_map/psum | solution.py:131
  170.3 1.8 convert_element_type.67
  172.1 8.1 %fusion.18 = f32[4096,1024]{1,0:T(8,128)} fusion(bf16[96,1024]{1,0:T(8,128)(2,1)S(1)} %copy-done.6, f32[4096,192]{0,1:T(8,128)S(1)} %convert_element_type.67), kind=kOutput, calls=%fused_computation.24 | convolution fusion | flops 807665664 | bytes 20119552 | tf_op jit(solution)/shard_map/dot_general | solution.py:137
  180.2 0.6 copy-done.14
  180.9 0.1 select_reduce_fusion
  181.0 339.7 %reduce-scatter.5.cloned.1.call-done = f32[64,1024]{1,0:T(8,128)} async-done(((f32[4096,1024]{1,0:T(8,128)}), f32[64,1024]{1,0:T(8,128)}) %reduce-scatter.5.cloned.1.call-update) | async-done | bytes 262160 | tf_op jit(solution)/shard_map/reduce_scatter | solution.py:136
  520.7 1.6 fusion.41
  522.4 81.9 %all_gather.7 = f32[1,131072]{1,0:T(1,128)S(1)} all-gather(f32[1,1024]{1,0:T(1,128)S(1)} %slice.36), channel_id=1, replica_groups=mesh['req'=64,'head'=2] {'req','head'}, dimensions={1}, use_global_device_ids=true | all-gather | bytes 528384 | tf_op jit(solution)/shard_map/all_gather | solution.py:145
  604.2 0.5 broadcast.162
  604.8 1.9 reduce.3
  606.7 0.1 multiply_reduce_fusion
  606.9 4.2 fusion.44
  611.1 63.7 %pmax.7 = f32[64]{0:T(128)S(1)} all-reduce(f32[64]{0:T(128)S(1)} %get-tuple-element.14), channel_id=1, replica_groups=mesh['req'=64,'head'=2] {'req','head'}, use_global_device_ids=true, to_apply=%region_13.14 | all-reduce | flops 64 | bytes 512 | tf_op jit(solution)/shard_map/pmax | solution.py:148
  674.8 0.2 exponential_reduce_fusion
  675.0 64.2 %psum.23 = f32[64]{0:T(128)S(1)} all-reduce(f32[64]{0:T(128)S(1)} %exponential_reduce_fusion), channel_id=1, replica_groups=mesh['req'=64,'head'=2] {'req','head'}, use_global_device_ids=true, to_apply=%region_15.16 | all-reduce | flops 64 | bytes 512 | tf_op jit(solution)/shard_map/psum | solution.py:149
  739.2 0.1 subtract_subtract_fusion
  739.3 0.7 gather_fusion
  740.0 0.8 broadcast_select_fusion
  (60 shorter events, 0.9 us)
Async XLA Ops:
  7.2 15.3 %copy-start = (bf16[2048,512]{1,0:T(8,128)(2,1)S(1)}, bf16[2048,512]{1,0:T(8,128)(2,1)}, u32[]{:S(2)}) copy-start(bf16[2048,512]{1,0:T(8,128)(2,1)} %param.21) | copy-start | bytes 6291460
  7.2 10.9 %copy-start.10 = (f32[128]{0:T(128)S(1)}, f32[128]{0:T(128)}, u32[]{:S(2)}) copy-start(f32[128]{0:T(128)} %param.23) | copy-start | bytes 1540
  7.2 44.5 %reduce-scatter.3.cloned.1.call-start = ((), (), s32[]{:S(2)}) async-start(), calls=%async_computation.2 | async-start | bytes 393216 | tf_op jit(solution)/shard_map/reduce_scatter | solution.py:118
  17.7 4.8 copy-start.2
  17.7 4.8 copy-start.7
  18.4 4.8 copy-start.11
  23.0 4.6 copy-start.3
  28.1 3.6 copy-start.4
  33.6 21.6 %copy-start.9 = (f32[1024]{0:T(1024)S(1)}, f32[1024]{0:T(1024)}, u32[]{:S(2)}) copy-start(f32[1024]{0:T(1024)} %param.30) | copy-start | bytes 12292
  33.6 103.0 %copy-start.12 = (bf16[1024,96]{0,1:T(8,128)(2,1)S(1)}, bf16[1024,96]{0,1:T(8,128)(2,1)}, u32[]{:S(2)}) copy-start(bf16[1024,96]{0,1:T(8,128)(2,1)} %param.32) | copy-start | bytes 589828
  33.7 103.0 %copy-start.13 = (bf16[1024,96]{0,1:T(8,128)(2,1)S(1)}, bf16[1024,96]{0,1:T(8,128)(2,1)}, u32[]{:S(2)}) copy-start(bf16[1024,96]{0,1:T(8,128)(2,1)} %param.31) | copy-start | bytes 589828
  37.5 99.2 %all-gather.2.cloned.1.call-start = ((), (), s32[]{:S(2)}) async-start(), calls=%async_computation.3 | async-start | bytes 8519680 | tf_op jit(solution)/shard_map/all_gather | solution.py:127
  56.9 113.5 %all-reduce.2.cloned.1.call-start = ((), (), s32[]{:S(2)}) async-start(), calls=%async_computation.4 | async-start | bytes 3145728 | tf_op jit(solution)/shard_map/psum | solution.py:131
  144.2 27.9 %copy-start.6 = (bf16[96,1024]{1,0:T(8,128)(2,1)S(1)}, bf16[96,1024]{1,0:T(8,128)(2,1)}, u32[]{:S(2)}) copy-start(bf16[96,1024]{1,0:T(8,128)(2,1)} %param.33) | copy-start | bytes 589828
  144.2 376.5 %reduce-scatter.5.cloned.1.call-start = ((), (), s32[]{:S(2)}) async-start(), calls=%async_computation.5 | async-start | bytes 17039360 | tf_op jit(solution)/shard_map/reduce_scatter | solution.py:136
  180.2 0.7 copy-start.14
  180.2 340.5 %copy-start.5 = (bf16[64,1024]{1,0:T(8,128)(2,1)S(1)}, bf16[64,1024]{1,0:T(8,128)(2,1)}, u32[]{:S(2)}) copy-start(bf16[64,1024]{1,0:T(8,128)(2,1)} %reduce-scatter.3.cloned.1.call-done) | copy-start | bytes 393220
  180.9 426.0 %copy-start.8 = (f32[2048]{0:T(1024)S(1)}, f32[2048]{0:T(1024)}, u32[]{:S(2)}) copy-start(f32[2048]{0:T(1024)} %param.34) | copy-start | bytes 24580
  606.9 133.9 %copy-start.1 = (bf16[2048,512]{1,0:T(8,128)(2,1)S(1)}, bf16[2048,512]{1,0:T(8,128)(2,1)}, u32[]{:S(2)}) copy-start(bf16[2048,512]{1,0:T(8,128)(2,1)} %param.21) | copy-start | bytes 6291460
Sparse Core Ops, SparseCore 0:
  37.6 13.9 reduce-scatter.2
  57.0 79.6 all-gather.1
  144.3 25.9 all-reduce.1
  180.4 340.3 reduce-scatter.4
where the time goes:
time: 748 us; the launch traced here: 747 us
  waiting for transfers between devices  460 us (61%)
  blocking collectives  212 us (28%)
  matrix products  33.1 us (4%)
  between operations  16.1 us (2%)
  local copies, waits for them, and re-layouts  13.3 us (2%)
  other arithmetic  12.9 us (2%)
    reduce_scatter x1, waiting for transfers between devices, on_device(): lax.psum_scatter(jnp.dot(active, w_down, preferred_element_type=jnp.float...  340 us
    all_gather x1, blocking collectives, on_device(): lax.all_gather(last_row, ('req', 'head'), axis=1, tiled=True).reshape(-1, D)  81.9 us
    all_gather x1, waiting for transfers between devices, on_device(): lax.all_gather(mixed_rows, 'req', axis=0, tiled=True)  79.7 us
    psum x1, blocking collectives, on_device(): lax.psum(jnp.sum(jnp.exp(logits - row_max[:, None]), axis=1), ('req', 'he...  64.2 us
    pmax x1, blocking collectives, on_device(): row_max = lax.pmax(jnp.max(logits, axis=1), ('req', 'head'))  63.7 us
    psum x1, waiting for transfers between devices, on_device(): lax.psum(partial_rows.astype(jnp.bfloat16), 'head').astype(jnp.float32)  26.1 us
  transfers between devices with their start and end apart: 4, of which 4 were waited for; matrix products, arithmetic and copies ran while one was open for 0% of the time, Pallas kernels for 0%

commit v1 on v0

v1 whole, which is shorter than its diff:
```python
import functools
import math

import jax
import jax.numpy as jnp
import numpy as np
from jax import lax
from jax.experimental import pallas as pl
from jax.experimental.pallas import tpu as pltpu
from jax.sharding import PartitionSpec as P

MESH = pl.DeviceIdType.MESH
F32, BF16 = jnp.float32, jnp.bfloat16

D = 2048
HEAD_DIM = 128
ROPE_BASE = 1000000.0
EPS = 1e-06
SHIFT = 4.0
LOG2E = math.log2(math.e)

SIDE = 4
ROWS = 64
HALF = ROWS // 2
PART = HALF // 2
UNITS = 96
PLANE_UNITS = SIDE * UNITS
KEYS = 2048
KEY_BLOCK = 512
VOC = 1187
VOC_BLOCK = 256
N_COPIES = 100


def nt_dot(a, b):
    return lax.dot_general(a, b, (((1,), (1,)), ((), ())), preferred_element_type=F32)


def nn_dot(a, b):
    return jnp.dot(a, b, preferred_element_type=F32)


def step_kernel(
    hidden, attn_gain, query_gain, key_gain, mlp_gain, final_gain, freq, order, order_s, lengths,
    w_query, w_key, w_value, w_out, cache_k, cache_v, w_gate, w_up, w_down, w_vocab,
    out, logp,
    normed, wq, wk, wv, wo, kc, vc, voc, wgu, wd, qs, kn, vn, att, proj, proj_in, gains, resid,
    rows, part, sh1, rh1, sf1, rf1, red, sh2, rh2, sf2, rf2, out_s, out_r,
    fr, final, st1, st2, st3, lsem, ssem, rsem,
):
    req = lax.axis_index("req")
    core = lax.axis_index("head")
    other = 1 - core
    y = req // (SIDE * SIDE)
    x = (req // SIDE) % SIDE
    z = req % SIDE

    def at(yy, xx, zz, cc):
        return ((yy % SIDE) * (SIDE * SIDE) + (xx % SIDE) * SIDE + (zz % SIDE), cc)

    along = {
        "y": lambda d: at(y + d + SIDE, x, z, core),
        "x": lambda d: at(y, x + d + SIDE, z, core),
        "z": lambda d: at(y, x, z + d + SIDE, core),
    }
    sibling = (req, other)
    counters = {"local": 0, "remote": 0}

    def local(src, dst):
        i = counters["local"]
        counters["local"] = i + 1
        return pltpu.make_async_copy(src, dst, lsem.at[i])

    def remote(src, dst, device):
        i = counters["remote"]
        counters["remote"] = i + 1
        return pltpu.make_async_remote_copy(
            src_ref=src, dst_ref=dst, send_sem=ssem.at[i], recv_sem=rsem.at[i],
            device_id=device, device_id_type=MESH,
        )

    sent = []

    def go(copies):
        for c in copies:
            c.start()
            sent.append(c)
        return copies

    def got(copies):
        for c in copies:
            c.wait_recv()

    load_k = local(w_key, wk)
    load_v = local(w_value, wv)
    load_q = local(w_query, wq)
    load_kc = local(cache_k.at[0], kc)
    load_vc = local(cache_v.at[0], vc)
    load_o = local(w_out, wo)
    load_voc = local(w_vocab, voc)

    def shard(zz, h):
        o = pl.multiple_of(zz * UNITS, UNITS)
        return [
            wgu.at[h, pl.ds(o, UNITS)],
            wgu.at[h, pl.ds(PLANE_UNITS + o, UNITS)],
            wd.at[pl.ds(o, UNITS), pl.ds(pl.multiple_of(h * (D // 2), D // 2), D // 2)],
        ]

    def half_shard(zz, h, k):
        n = UNITS // 2
        return [r.at[pl.ds(k * n, n)] for r in shard(zz, h)]

    own = [w_gate, w_up, w_down]
    load_own = [local(s, d) for s, d in zip(own, shard(z, core))]
    load_gain = local(mlp_gain, gains.at[pl.ds(pl.multiple_of(core * 8, 8), 8)])
    for c in [load_k, load_v, load_q]:
        c.start()
    for c in load_own + [load_gain]:
        c.start()

    barrier = pltpu.get_barrier_semaphore()
    peers = [sibling]
    for d in (1, 2, 3):
        peers += [along["x"](d), along["y"](d), at(y, x, z + d, core), at(y, x, z + d, other)]
    for p in peers:
        pl.semaphore_signal(barrier, inc=1, device_id=p, device_id_type=MESH)
    pl.semaphore_wait(barrier, len(peers))

    zc = z
    zm, zp, zo = (z + 3) % SIDE, (z + 1) % SIDE, (z + 2) % SIDE
    w_up1 = go([remote(s, d, along["z"](1)) for s, d in zip(own, shard(zc, core))])
    w_dn1 = go([remote(s, d, along["z"](-1)) for s, d in zip(own, shard(zc, core))])
    gain_x = go([remote(mlp_gain, gains.at[pl.ds(pl.multiple_of(core * 8, 8), 8)], sibling)])
    w_sib = go([remote(s, d, sibling) for s, d in zip(own, shard(zc, core))])
    for c in [load_kc, load_vc, load_o]:
        c.start()

    tokens = hidden[...].astype(F32)
    scale = lax.rsqrt(jnp.mean(tokens * tokens, axis=-1, keepdims=True) + EPS)
    normed[...] = (tokens * scale * attn_gain[...]).astype(BF16)
    slot = order_s[req]
    length = lengths[slot]
    position = (length + lax.broadcasted_iota(jnp.int32, (ROWS, 1), 0)).astype(F32)
    angle = position * freq[...]
    cosine = jnp.cos(angle)
    lane = lax.broadcasted_iota(jnp.int32, (ROWS, HEAD_DIM), 1)
    sine = jnp.where(lane < HEAD_DIM // 2, -jnp.sin(angle), jnp.sin(angle))

    def rotated(v, gain):
        v = v * lax.rsqrt(jnp.mean(v * v, axis=-1, keepdims=True) + EPS) * gain
        return (v * cosine + pltpu.roll(v, HEAD_DIM // 2, 1) * sine).astype(BF16)

    load_k.wait()
    for j in range(2):
        both = nn_dot(normed[...], wk[:, j * 256 : (j + 1) * 256])
        for i in range(2):
            kn[2 * j + i] = rotated(both[:, i * 128 : (i + 1) * 128], key_gain[...])
    load_v.wait()
    for j in range(2):
        vn[:, j * 256 : (j + 1) * 256] = nn_dot(
            normed[...], wv[:, j * 256 : (j + 1) * 256]
        ).astype(BF16)
    load_q.wait()
    for j in range(4):
        both = nn_dot(normed[...], wq[:, j * 256 : (j + 1) * 256])
        for i in range(2):
            qs[j, i * ROWS : (i + 1) * ROWS] = rotated(
                both[:, i * 128 : (i + 1) * 128], query_gain[...]
            )

    load_kc.wait()
    load_vc.wait()
    load_voc.start()
    slope = LOG2E / math.sqrt(HEAD_DIM)
    base = SHIFT * LOG2E
    row_at = lax.broadcasted_iota(jnp.int32, (2 * ROWS, ROWS), 0) % ROWS
    causal = row_at >= lax.broadcasted_iota(jnp.int32, (2 * ROWS, ROWS), 1)

    def one_head(g):
        q = qs[g]
        cols = pl.ds(pl.multiple_of(g * HEAD_DIM, HEAD_DIM), HEAD_DIM)
        fresh = jnp.where(causal, jnp.exp2(nt_dot(q, kn[g]) * slope - base), 0.0)
        total = jnp.sum(fresh, axis=1, keepdims=True)
        acc = nn_dot(fresh.astype(BF16), vn[:, cols])
        for b in range(KEYS // KEY_BLOCK):
            span = slice(b * KEY_BLOCK, (b + 1) * KEY_BLOCK)
            s = nt_dot(q, kc[span, cols])
            key_at = b * KEY_BLOCK + lax.broadcasted_iota(jnp.int32, s.shape, 1)
            p = jnp.where(key_at < length, jnp.exp2(s * slope - base), 0.0)
            total = total + jnp.sum(p, axis=1, keepdims=True)
            acc = acc + nn_dot(p.astype(BF16), vc[span, cols])
        done = (acc / total).astype(BF16)
        att[:, pl.ds(pl.multiple_of(2 * g * HEAD_DIM, HEAD_DIM), HEAD_DIM)] = done[:ROWS]
        att[:, pl.ds(pl.multiple_of((2 * g + 1) * HEAD_DIM, HEAD_DIM), HEAD_DIM)] = done[ROWS:]

    one_head(0)
    one_head(1)

    got(w_up1)
    w_up2 = go([
        remote(r, r, along["z"](1)) for r in half_shard(zm, core, 0)
    ])
    w_sib_m = go([remote(r, r, sibling) for r in shard(zm, core)])
    got(w_dn1)
    w_dn2 = go([
        remote(r, r, along["z"](-1)) for r in half_shard(zp, core, 1)
    ])
    w_sib_p = go([remote(r, r, sibling) for r in shard(zp, core)])

    one_head(2)
    one_head(3)

    load_o.wait()
    for j in range(4):
        cols = slice(j * 512, (j + 1) * 512)
        proj[:, cols] = nn_dot(att[...], wo[:, cols])

    mine = pl.ds(pl.multiple_of(core * HALF, HALF), HALF)
    theirs = pl.ds(pl.multiple_of(other * HALF, HALF), HALF)
    proj_x = go([remote(proj.at[theirs], proj_in, sibling)])
    got(w_up2 + w_dn2)
    w_sib_o = go([remote(r, r, sibling) for r in shard(zo, core)])
    got(gain_x)
    load_gain.wait()
    got(proj_x)
    r = hidden[mine].astype(F32) + (proj[mine] + proj_in[...])
    resid[...] = r
    scale = lax.rsqrt(jnp.mean(r * r, axis=-1, keepdims=True) + EPS)
    for j in range(D // 128):
        cols = slice(j * 128, (j + 1) * 128)
        mixed = (r[:, cols] * scale * gains[j : j + 1]).astype(BF16)
        rows[0, y, x, :, cols] = mixed[:PART]
        rows[1, x, y, :, cols] = mixed[PART:]

    inner, outer = ("x", "y"), ("y", "x")
    inner_at, outer_at = (x, y), (y, x)

    def ring_start(block, p, axis):
        return go([
            remote(block(p), block(p), along[axis](1)),
            remote(block(p), block(p), along[axis](-1)),
        ])

    def ring_pass(block, p, axis, first):
        lo = slice(0, D // 2), slice(D // 2, D)

        def half(pos, k):
            b = block(pos)
            return b.at[..., pl.ds(k * (D // 2), D // 2)]

        got(first[:1])
        a = go([remote(half((p + 3) % SIDE, 0), half((p + 3) % SIDE, 0), along[axis](1))])
        got(first[1:])
        b = go([remote(half((p + 1) % SIDE, 1), half((p + 1) % SIDE, 1), along[axis](-1))])
        return a + b

    def small(s):
        return lambda pos: rows.at[s, outer_at[s], pos]

    def large(s):
        return lambda pos: rows.at[s, pos]

    one = [ring_start(small(s), inner_at[s], inner[s]) for s in range(2)]
    two = [ring_pass(small(s), inner_at[s], inner[s], one[s]) for s in range(2)]
    three = []
    for s in range(2):
        got(two[s])
        three.append(ring_start(large(s), outer_at[s], outer[s]))
    four = [ring_pass(large(s), outer_at[s], outer[s], three[s]) for s in range(2)]

    for c in load_own:
        c.wait()
    got(w_sib + w_sib_m + w_sib_p + w_sib_o)

    def feed(s):
        xa = rows[s].reshape(SIDE * SIDE * PART, D)
        gu = nt_dot(xa[:, : D // 2], wgu[0]) + nt_dot(xa[:, D // 2 :], wgu[1])
        gate, up = gu[:, :PLANE_UNITS], gu[:, PLANE_UNITS:]
        active = (gate / (1.0 + jnp.exp(-gate)) * up).astype(BF16)
        for j in range(4):
            cols = slice(j * 512, (j + 1) * 512)
            part[s, :, :, :, cols] = nn_dot(active, wd[:, cols]).reshape(SIDE, SIDE, PART, 512)

    def reduce_start(s, stage, axis, p, block, sh, rh):
        far = block((p + 2) % SIDE)
        sh[s, 0] = far[..., : D // 2].astype(BF16)
        sh[s, 1] = far[..., D // 2 :].astype(BF16)
        return go([
            remote(sh.at[s, 0], rh.at[s, 0], along[axis](1)),
            remote(sh.at[s, 1], rh.at[s, 1], along[axis](-1)),
        ])

    def reduce_pass(s, axis, p, block, rh, sf, rf, first):
        nxt = block((p + 1) % SIDE)
        prv = block((p + 3) % SIDE)
        sf[s, 0, ..., D // 2 :] = nxt[..., D // 2 :].astype(BF16)
        sf[s, 1, ..., : D // 2] = prv[..., : D // 2].astype(BF16)
        got(first[:1])
        sf[s, 0, ..., : D // 2] = (nxt[..., : D // 2] + rh[s, 0].astype(F32)).astype(BF16)
        a = go([remote(sf.at[s, 0], rf.at[s, 0], along[axis](1))])
        got(first[1:])
        sf[s, 1, ..., D // 2 :] = (prv[..., D // 2 :] + rh[s, 1].astype(F32)).astype(BF16)
        b = go([remote(sf.at[s, 1], rf.at[s, 1], along[axis](-1))])
        return a + b

    def reduce_end(s, p, block, rf, second):
        got(second)
        return block(p) + rf[s, 0].astype(F32) + rf[s, 1].astype(F32)

    def p1(s):
        return lambda pos: part[s, pos]

    def p2(s):
        return lambda pos: red[s, pos]

    five = []
    for s in range(2):
        got(four[s])
        feed(s)
        five.append(reduce_start(s, 1, outer[s], outer_at[s], p1(s), sh1, rh1))
    six = [
        reduce_pass(s, outer[s], outer_at[s], p1(s), rh1, sf1, rf1, five[s]) for s in range(2)
    ]
    seven = []
    for s in range(2):
        red[s] = reduce_end(s, outer_at[s], p1(s), rf1, six[s])
        seven.append(reduce_start(s, 2, inner[s], inner_at[s], p2(s), sh2, rh2))
    eight = [
        reduce_pass(s, inner[s], inner_at[s], p2(s), rh2, sf2, rf2, seven[s]) for s in range(2)
    ]
    for s in range(2):
        span = slice(s * PART, (s + 1) * PART)
        resid[span] = resid[span] + reduce_end(s, inner_at[s], p2(s), rf2, eight[s])

    def slot_rows(first, count):
        return fr.at[pl.ds(pl.multiple_of(first * 16, 16), count * 16)]

    last_z = [remote(slot_rows(x * SIDE + z, 1), slot_rows(x * SIDE + z, 1), along["z"](d)) for d in (1, 2, 3)]
    last_x = [remote(slot_rows(x * SIDE, SIDE), slot_rows(x * SIDE, SIDE), along["x"](d)) for d in (1, 2, 3)]
    last_y = [remote(final.at[y], final.at[y], along["y"](d)) for d in (1, 2, 3)]
    last_c = [remote(final.at[(y + d) % SIDE], final.at[(y + d) % SIDE], sibling) for d in (0, 3, 2, 1)]

    @pl.when(core == 1)
    def _():
        row = resid[HALF - 1 : HALF]
        row = row * lax.rsqrt(jnp.mean(row * row, axis=-1, keepdims=True) + EPS) * final_gain[...]
        row = row.astype(BF16).astype(F32)
        at_row = pl.multiple_of((x * SIDE + z) * 16, 16)
        tile = jnp.concatenate([row[:, j * 128 : (j + 1) * 128] for j in range(16)], axis=0)
        fr[pl.ds(at_row, 16)] = tile
        for c in last_z:
            c.start()
        for c in last_z:
            c.wait()
        for c in last_x:
            c.start()
        for c in last_x:
            c.wait()
        for j in range(16):
            final[y, :, j * 128 : (j + 1) * 128] = fr[pl.ds(j, 16, stride=16)].astype(BF16)
        for c in last_y:
            c.start()
        last_c[0].start()
        for d in (1, 2, 3):
            last_y[d - 1].wait_recv()
            last_c[d].start()
        for c in last_y + last_c:
            c.wait_send()

    keep = pl.ds(pl.multiple_of(core * (D // 2), D // 2), D // 2)
    give = pl.ds(pl.multiple_of(other * (D // 2), D // 2), D // 2)
    out_s[...] = resid[:, give].astype(BF16)
    out_x = go([remote(out_s, out_r, sibling)])
    out[mine] = resid[:, keep].astype(BF16)

    @pl.when(core == 0)
    def _():
        for c in last_c:
            c.wait_recv()

    load_voc.wait()
    pick = (
        order[...] == lax.broadcasted_iota(jnp.int32, (ROWS, ROWS), 0)
    ).astype(BF16)
    final_rows = nn_dot(pick, final[...].reshape(ROWS, D)).astype(BF16)
    top = None
    for start in range(0, VOC, VOC_BLOCK):
        stop = min(start + VOC_BLOCK, VOC)
        part_l = nt_dot(final_rows, voc[start:stop])
        logp[:, start:stop] = part_l
        m = jnp.max(part_l, axis=1, keepdims=True)
        top = m if top is None else jnp.maximum(top, m)
    total = jnp.sum(jnp.exp(logp[...] - top), axis=1, keepdims=True)

    eye = lax.broadcasted_iota(jnp.int32, (ROWS, ROWS), 0) == lax.broadcasted_iota(
        jnp.int32, (ROWS, ROWS), 1
    )

    def as_row(col):
        return jnp.sum(jnp.where(eye, col, 0.0), axis=0, keepdims=True)

    def exchange(buf, index, devices):
        copies = go([remote(buf.at[index], buf.at[index], d) for d in devices])
        got(copies)
        m = jnp.max(buf[:, 0, :ROWS], axis=0, keepdims=True)
        t = jnp.sum(buf[:, 1, :ROWS] * jnp.exp(buf[:, 0, :ROWS] - m), axis=0, keepdims=True)
        return m, t

    def put(buf, index, m, t):
        buf[index, 0:1, :ROWS] = m
        buf[index, 1:2, :ROWS] = t

    put(st1, z * 2 + core, as_row(top), as_row(total))
    m, t = exchange(
        st1, z * 2 + core,
        [sibling] + [at(y, x, z + d, c) for d in (1, 2, 3) for c in (core, other)],
    )
    put(st2, x, m, t)
    m, t = exchange(st2, x, [along["x"](d) for d in (1, 2, 3)])
    put(st3, y, m, t)
    m, t = exchange(st3, y, [along["y"](d) for d in (1, 2, 3)])
    top = jnp.sum(jnp.where(eye, m, 0.0), axis=1, keepdims=True)
    log_total = jnp.sum(jnp.where(eye, jnp.log(t), 0.0), axis=1, keepdims=True)
    logp[...] = logp[...] - top - log_total

    got(out_x)
    out[theirs] = out_r[...]
    for c in sent:
        c.wait_send()


def on_device(
    hidden_in, attn_gain, w_query, w_key, w_value, query_gain, key_gain, w_out,
    cache_keys, cache_values, cache_lengths, slot_request, mlp_gain, w_gate, w_up, w_down,
    final_gain, w_vocab,
):
    half_dim = HEAD_DIM // 2
    one = ROPE_BASE ** (-2.0 * np.arange(half_dim) / HEAD_DIM)
    freq = jnp.asarray(np.concatenate([one, one])[None].astype(np.float32))
    vmem = pl.BlockSpec(memory_space=pltpu.VMEM)
    smem = pl.BlockSpec(memory_space=pltpu.SMEM)
    far = pl.BlockSpec(memory_space=pl.ANY)
    V = pltpu.VMEM
    S = SIDE
    return pl.pallas_call(
        step_kernel,
        out_shape=(
            jax.ShapeDtypeStruct((ROWS, D // 2), BF16),
            jax.ShapeDtypeStruct((ROWS, VOC), F32),
        ),
        in_specs=[vmem] * 8 + [smem] * 2 + [far] * 10,
        out_specs=(vmem, vmem),
        scratch_shapes=[
            V((ROWS, D), BF16),
            V((D, 1024), BF16), V((D, 512), BF16), V((D, 512), BF16), V((1024, D), BF16),
            V((KEYS, 512), BF16), V((KEYS, 512), BF16), V((VOC, D), BF16),
            V((2, 2 * PLANE_UNITS, D // 2), BF16), V((PLANE_UNITS, D), BF16),
            V((4, 2 * ROWS, HEAD_DIM), BF16), V((4, ROWS, HEAD_DIM), BF16), V((ROWS, 512), BF16),
            V((ROWS, 1024), BF16), V((ROWS, D), F32), V((HALF, D), F32), V((16, 128), F32),
            V((HALF, D), F32),
            V((2, S, S, PART, D), BF16), V((2, S, S, PART, D), F32),
            V((2, 2, S, PART, D // 2), BF16), V((2, 2, S, PART, D // 2), BF16),
            V((2, 2, S, PART, D), BF16), V((2, 2, S, PART, D), BF16),
            V((2, S, PART, D), F32),
            V((2, 2, PART, D // 2), BF16), V((2, 2, PART, D // 2), BF16),
            V((2, 2, PART, D), BF16), V((2, 2, PART, D), BF16),
            V((HALF, D // 2), BF16), V((HALF, D // 2), BF16),
            V((S * S * 16, 128), F32), V((S, S * S, D), BF16),
            V((2 * S, 8, 128), F32), V((S, 8, 128), F32), V((S, 8, 128), F32),
            pltpu.SemaphoreType.DMA((16,)),
            pltpu.SemaphoreType.DMA((N_COPIES,)),
            pltpu.SemaphoreType.DMA((N_COPIES,)),
        ],
        compiler_params=pltpu.CompilerParams(
            collective_id=0, has_side_effects=True, vmem_limit_bytes=58 * 1024 * 1024
        ),
    )(
        hidden_in, attn_gain.reshape(1, D), query_gain.reshape(1, HEAD_DIM),
        key_gain.reshape(1, HEAD_DIM), mlp_gain.reshape(8, 128), final_gain.reshape(1, D), freq,
        slot_request.reshape(1, ROWS), slot_request, cache_lengths,
        w_query, w_key, w_value, w_out, cache_keys, cache_values,
        w_gate.T, w_up.T, w_down, w_vocab.T,
    )


def solution(mesh):
    in_specs = (
        P("req", None), P(), P(None, "head"), P(None, "head"), P(None, "head"), P(), P(),
        P("head", None), P("req", None, "head"), P("req", None, "head"), P(), P(), P("head"),
        P("head", "req"), P("head", "req"), P("req", "head"), P(), P(None, ("req", "head")),
    )
    out_specs = (P("req", "head"), P(None, ("req", "head")))
    return jax.shard_map(
        on_device, mesh=mesh, in_specs=in_specs, out_specs=out_specs, check_vma=False
    )
```

time: 748 us -> 95.7 us (0.13)
  waiting for transfers between devices: 460 us -> 0 us
  blocking collectives: 212 us -> 0 us
  Pallas kernels: 0 us -> 90.8 us
  matrix products: 33.1 us -> 0 us
  between operations: 16.1 us -> 0.65 us
  other arithmetic: 12.9 us -> 0 us
  local copies, waits for them, and re-layouts: 13.3 us -> 3.29 us
    reduce_scatter x2 -> x0, waiting for transfers between devices: 354 us -> none  [the longest x1 340 us: on_device(): lax.psum_scatter(jnp.dot(active, w_down, preferred_element_type=jnp.float...]
    pallas_call x0 -> x1, Pallas kernels: none -> 90.8 us  [on_device(): pl.pallas_call(step_kernel, out_shape=(jax.ShapeDtypeStruct((ROWS, D // 2...]
    all_gather x1 -> x0, blocking collectives: 81.9 us -> none  [on_device(): lax.all_gather(last_row, ('req', 'head'), axis=1, tiled=True).reshape(-1, D)]
    all_gather x1 -> x0, waiting for transfers between devices: 79.7 us -> none  [on_device(): lax.all_gather(mixed_rows, 'req', axis=0, tiled=True)]
    psum x2 -> x0, blocking collectives: 66.6 us -> none  [the longest x1 64.2 us: on_device(): lax.psum(jnp.sum(jnp.exp(logits - row_max[:, None]), axis=1), ('req', 'he...]
    pmax x1 -> x0, blocking collectives: 63.7 us -> none  [on_device(): row_max = lax.pmax(jnp.max(logits, axis=1), ('req', 'head'))]
    dot_general x11 -> x0, matrix products: 33.1 us -> none  [the longest x1 8.12 us: on_device(): jnp.dot(active, w_down, preferred_element_type=jnp.float32)]
    psum x1 -> x0, waiting for transfers between devices: 26.1 us -> none  [on_device(): lax.psum(partial_rows.astype(jnp.bfloat16), 'head').astype(jnp.float32)]
  transfers between devices with their start and end apart: 4 -> 0, of which waited for: 4 -> 0; matrix products, arithmetic and copies ran while one was open for 0% -> 0% of each run, Pallas kernels for 0% -> 0%
where the time goes in v1:
time: 95.7 us; the launch traced here: 94.8 us
  Pallas kernels  90.8 us (95%)
  local copies, waits for them, and re-layouts  3.29 us (3%)
    pallas_call x1, Pallas kernels, on_device(): pl.pallas_call(step_kernel, out_shape=(jax.ShapeDtypeStruct((ROWS, D // 2...  90.8 us
    unnamed x2, local copies, waits for them, and re-layouts  3.29 us

profile of v1, /device:TPU:1, one launch (start us, length us, event | category | flops | bytes accessed | tf_op | source)
XLA Modules:
  0.0 94.8 jit_solution(6648366759768293847)
XLA Ops:
  0.6 90.8 %shard_map.194 = (bf16[64,1024]{1,0:T(8,128)(2,1)}, f32[64,1187]{1,0:T(8,128)}) custom-call(bf16[64,2048]{1,0:T(8,128)(2,1)} %hidden.1, f32[1,2048]{1,0:T(1,128)} %bitcast.12, f32[1,128]{1,0:T(1,128)} %bitcast.16, f32[1,128]{1,0:T(1,128)} %bitcast.17, f32[8,128]{1,0:T(8,128)} %bitcast.14, f32[1,2048]{1,0:T(1,128)} %bitcast.13, f32[1,128]{1,0:T(1,128)} %constant.2.clone.freq, ...), custom_call_target="tpu_custom_call" | custom-call | tf_op jit(solution)/shard_map/pallas_call | solution.py:446
  91.5 1.6 %copy.23 = bf16[64,1024]{1,0:T(8,128)(2,1)} copy(bf16[64,1024]{1,0:T(8,128)(2,1)} %get-tuple-element.4) | data formatting | bytes 262144
  93.0 1.7 %copy.24 = f32[64,1187]{1,0:T(8,128)} copy(f32[64,1187]{1,0:T(8,128)} %get-tuple-element.5) | data formatting | bytes 607744

commit v2 on v1

v2 whole, which is shorter than its diff:
```python
import functools
import math

import jax
import jax.numpy as jnp
import numpy as np
from jax import lax
from jax.experimental import pallas as pl
from jax.experimental.pallas import tpu as pltpu
from jax.sharding import PartitionSpec as P

MESH = pl.DeviceIdType.MESH
F32, BF16 = jnp.float32, jnp.bfloat16

D = 2048
HEAD_DIM = 128
ROPE_BASE = 1000000.0
EPS = 1e-06
SHIFT = 4.0
LOG2E = math.log2(math.e)

SIDE = 4
ROWS = 64
HALF = ROWS // 2
PART = HALF // 2
UNITS = 96
PLANE_UNITS = SIDE * UNITS
KEYS = 2048
KEY_BLOCK = 512
VOC = 1187
VOC_BLOCK = 256
N_COPIES = 100


def nt_dot(a, b):
    return lax.dot_general(a, b, (((1,), (1,)), ((), ())), preferred_element_type=F32)


def nn_dot(a, b):
    return jnp.dot(a, b, preferred_element_type=F32)


def step_kernel(
    hidden, attn_gain, query_gain, key_gain, mlp_gain, final_gain, freq, order, order_s, lengths,
    w_query, w_key, w_value, w_out, cache_k, cache_v, w_gate, w_up, w_down, w_vocab,
    out, logp,
    normed, wq, wk, wv, wo, kc, vc, voc, wf, qs, kn, vn, att, proj, proj_in, gains, resid,
    rows, part, in1, mid, in2, out_s, out_r,
    last_a, last_p, last_in, last_b, last_res, spread, last_x, stats,
    lsem, ssem, rsem, gsem, plane_sem, all_sem,
):
    req = lax.axis_index("req")
    core = lax.axis_index("head")
    other = 1 - core
    y = req // (SIDE * SIDE)
    x = (req // SIDE) % SIDE
    z = req % SIDE

    def at(yy, xx, zz, cc):
        return ((yy % SIDE) * (SIDE * SIDE) + (xx % SIDE) * SIDE + (zz % SIDE), cc)

    along = {
        "y": lambda d: at(y + d, x, z, core),
        "x": lambda d: at(y, x + d, z, core),
        "z": lambda d: at(y, x, z + d, core),
    }
    sibling = (req, other)
    counters = {"local": 0, "remote": 0}

    def local(src, dst):
        i = counters["local"]
        counters["local"] = i + 1
        return pltpu.make_async_copy(src, dst, lsem.at[i])

    def remote(src, dst, device):
        i = counters["remote"]
        counters["remote"] = i + 1
        return pltpu.make_async_remote_copy(
            src_ref=src, dst_ref=dst, send_sem=ssem.at[i], recv_sem=rsem.at[i],
            device_id=device, device_id_type=MESH,
        )

    sent = []

    def go(copies):
        for c in copies:
            c.start()
            sent.append(c)
        return copies

    def got(copies):
        for c in copies:
            c.wait_recv()

    load_k = local(w_key, wk)
    load_v = local(w_value, wv)
    load_q = local(w_query, wq)
    load_kc = local(cache_k.at[0], kc)
    load_vc = local(cache_v.at[0], vc)
    load_o = local(w_out, wo)
    load_voc = local(w_vocab, voc)
    unit_at = pl.multiple_of(z * UNITS, UNITS)
    load_own = [
        local(w, wf.at[core, k, pl.ds(unit_at, UNITS)]) for k, w in enumerate((w_gate, w_up, w_down))
    ]
    my_gain = gains.at[pl.ds(pl.multiple_of(core * 8, 8), 8)]
    load_gain = local(mlp_gain, my_gain)
    for c in [load_k, load_v, load_q] + load_own + [load_gain, load_kc, load_vc, load_o]:
        c.start()

    barrier = pltpu.get_barrier_semaphore()
    peers = [sibling]
    for d in (1, 2, 3):
        peers += [along["x"](d), at(y, x + d, z, other), along["y"](d), along["z"](d)]
    for p in peers:
        pl.semaphore_signal(barrier, inc=1, device_id=p, device_id_type=MESH)

    tokens = hidden[...].astype(F32)
    scale = lax.rsqrt(jnp.mean(tokens * tokens, axis=-1, keepdims=True) + EPS)
    normed[...] = (tokens * scale * attn_gain[...]).astype(BF16)
    slot = order_s[req]
    length = lengths[slot]
    position = (length + lax.broadcasted_iota(jnp.int32, (ROWS, 1), 0)).astype(F32)
    angle = position * freq[...]
    cosine = jnp.cos(angle)
    lane = lax.broadcasted_iota(jnp.int32, (ROWS, HEAD_DIM), 1)
    sine = jnp.where(lane < HEAD_DIM // 2, -jnp.sin(angle), jnp.sin(angle))

    def rotated(v, gain):
        v = v * lax.rsqrt(jnp.mean(v * v, axis=-1, keepdims=True) + EPS) * gain
        return (v * cosine + pltpu.roll(v, HEAD_DIM // 2, 1) * sine).astype(BF16)

    load_k.wait()
    for j in range(2):
        both = nn_dot(normed[...], wk[:, j * 256 : (j + 1) * 256])
        for i in range(2):
            kn[2 * j + i] = rotated(both[:, i * 128 : (i + 1) * 128], key_gain[...])
    load_v.wait()
    for j in range(2):
        vn[:, j * 256 : (j + 1) * 256] = nn_dot(
            normed[...], wv[:, j * 256 : (j + 1) * 256]
        ).astype(BF16)

    def shard(zz, h):
        return wf.at[h, :, pl.ds(pl.multiple_of(zz * UNITS, UNITS), UNITS)]

    def half_shard(zz, h, k):
        n = UNITS // 2
        return wf.at[h, :, pl.ds(pl.multiple_of(zz * UNITS + k * n, n), n)]

    zm, zp, zo = (z + 3) % SIDE, (z + 1) % SIDE, (z + 2) % SIDE
    for c in load_own + [load_gain]:
        c.wait()
    pl.semaphore_wait(barrier, len(peers))
    w_first, w_second = [], []
    for copies, k_up in ((w_first, 0), (w_second, 1)):
        copies += go([
            remote(half_shard(z, core, k_up), half_shard(z, core, k_up), along["z"](1)),
            remote(half_shard(z, core, 1 - k_up), half_shard(z, core, 1 - k_up), along["z"](-1)),
        ])
    gain_x = go([remote(my_gain, my_gain, sibling)])
    w_sib = go([remote(shard(z, core), shard(z, core), sibling)])
    for d in (1, 2, 3):
        pl.semaphore_signal(plane_sem, inc=1, device_id=along["y"](d), device_id_type=MESH)

    load_q.wait()
    for j in range(4):
        both = nn_dot(normed[...], wq[:, j * 256 : (j + 1) * 256])
        for i in range(2):
            qs[j, i * ROWS : (i + 1) * ROWS] = rotated(
                both[:, i * 128 : (i + 1) * 128], query_gain[...]
            )

    load_kc.wait()
    load_vc.wait()
    load_voc.start()
    slope = LOG2E / math.sqrt(HEAD_DIM)
    base = SHIFT * LOG2E
    row_at = lax.broadcasted_iota(jnp.int32, (2 * ROWS, ROWS), 0) % ROWS
    causal = row_at >= lax.broadcasted_iota(jnp.int32, (2 * ROWS, ROWS), 1)

    def one_head(g):
        q = qs[g]
        cols = slice(g * HEAD_DIM, (g + 1) * HEAD_DIM)
        fresh = jnp.where(causal, jnp.exp2(nt_dot(q, kn[g]) * slope - base), 0.0)
        total = jnp.sum(fresh, axis=1, keepdims=True)
        acc = nn_dot(fresh.astype(BF16), vn[:, cols])
        for b in range(KEYS // KEY_BLOCK):
            span = slice(b * KEY_BLOCK, (b + 1) * KEY_BLOCK)
            s = nt_dot(q, kc[span, cols])
            key_at = b * KEY_BLOCK + lax.broadcasted_iota(jnp.int32, s.shape, 1)
            p = jnp.where(key_at < length, jnp.exp2(s * slope - base), 0.0)
            total = total + jnp.sum(p, axis=1, keepdims=True)
            acc = acc + nn_dot(p.astype(BF16), vc[span, cols])
        done = (acc / total).astype(BF16)
        att[:, 2 * g * HEAD_DIM : (2 * g + 1) * HEAD_DIM] = done[:ROWS]
        att[:, (2 * g + 1) * HEAD_DIM : (2 * g + 2) * HEAD_DIM] = done[ROWS:]

    for g in range(4):
        one_head(g)

    load_o.wait()
    for j in range(4):
        cols = slice(j * 512, (j + 1) * 512)
        proj[:, cols] = nn_dot(att[...], wo[:, cols])
    mine = pl.ds(pl.multiple_of(core * HALF, HALF), HALF)
    theirs = pl.ds(pl.multiple_of(other * HALF, HALF), HALF)
    proj_x = go([remote(proj.at[theirs], proj_in, sibling)])
    pl.semaphore_wait(plane_sem, 3)
    for d in (1, 2, 3):
        pl.semaphore_signal(all_sem, inc=1, device_id=along["z"](d), device_id_type=MESH)
    got(gain_x + proj_x)
    r = hidden[mine].astype(F32) + (proj[mine] + proj_in[...])
    resid[...] = r
    scale = lax.rsqrt(jnp.mean(r * r, axis=-1, keepdims=True) + EPS)
    for j in range(D // 128):
        cols = slice(j * 128, (j + 1) * 128)
        mixed = (r[:, cols] * scale * gains[j : j + 1]).astype(BF16)
        rows[0, y, x, :, cols] = mixed[:PART]
        rows[1, x, y, :, cols] = mixed[PART:]

    inner, outer = ("x", "y"), ("y", "x")
    inner_at, outer_at = (x, y), (y, x)
    hops = (2, 1, 3)

    def piece(s, o, i):
        return rows.at[s, o % SIDE, i % SIDE]

    def push(s, i, axis):
        b = piece(s, outer_at[s], i)
        return {d: go([remote(b, b, along[axis](d))])[0] for d in hops}

    one = [push(s, inner_at[s], inner[s]) for s in range(2)]
    two = [{0: push(s, inner_at[s], outer[s])} for s in range(2)]

    def each_chip(body):
        def step(d, carry):
            body(lax.rem(req + d, SIDE * SIDE * SIDE))
            return carry

        lax.fori_loop(1, SIDE**3, step, 0)

    def all_but_one(buf, n, k):
        return pltpu.make_async_remote_copy(
            src_ref=buf.at[pl.ds(0, n)], dst_ref=buf.at[pl.ds(0, n)],
            send_sem=gsem.at[k], recv_sem=gsem.at[k + 1], device_id=sibling, device_id_type=MESH,
        )

    def to_chip(src, dst, q, k):
        pltpu.make_async_remote_copy(
            src_ref=src, dst_ref=dst, send_sem=gsem.at[k], recv_sem=gsem.at[k + 1],
            device_id=(q, core), device_id_type=MESH,
        ).start()

    pl.semaphore_wait(all_sem, 3)
    chips = SIDE**3

    @pl.when(core == 1)
    def _():
        tile = jnp.concatenate(
            [resid[HALF - 1 : HALF, j * 128 : (j + 1) * 128] for j in range(16)], axis=0
        )
        last_res[...] = tile
        power = jnp.sum(jnp.sum(tile * tile, axis=1, keepdims=True), axis=0, keepdims=True)
        last_a[req] = (tile * lax.rsqrt(power / D + EPS) * gains[...]).astype(BF16)
        each_chip(lambda q: to_chip(last_a.at[req], last_a.at[req], q, 0))

    got(w_first)
    w_on = go([
        remote(half_shard(zm, core, 0), half_shard(zm, core, 0), along["z"](1)),
        remote(half_shard(zp, core, 1), half_shard(zp, core, 1), along["z"](-1)),
    ])

    for d in (1, 3, 2):
        for s in range(2):
            one[s][d].wait_recv()
            two[s][d] = push(s, inner_at[s] - d + SIDE, outer[s])
    got(w_second)
    w_sib += go([remote(shard(zm, core), shard(zm, core), sibling)])
    w_sib += go([remote(shard(zp, core), shard(zp, core), sibling)])

    def unpack(tiles):
        spread[...] = tiles[...].astype(F32).reshape(chips * 16, 128)
        for j in range(16):
            last_x[:, j * 128 : (j + 1) * 128] = spread[pl.ds(j, chips, stride=16)].astype(BF16)

    got(w_sib[:1])

    @pl.when(core == 1)
    def _():
        all_but_one(last_a, chips - 1, 0).wait_recv()
        unpack(last_a)
        units = pl.ds(unit_at, UNITS)
        lo, hi = last_x[:, : D // 2], last_x[:, D // 2 :]
        gate = nt_dot(lo, wf[0, 0, units]) + nt_dot(hi, wf[1, 0, units])
        up = nt_dot(lo, wf[0, 1, units]) + nt_dot(hi, wf[1, 1, units])
        active = (gate / (1.0 + jnp.exp(-gate)) * up).astype(BF16)
        for h in range(2):
            down = nn_dot(active, wf[h, 2, units])
            for j in range(8):
                spread[pl.ds(8 * h + j, chips, stride=16)] = down[:, j * 128 : (j + 1) * 128]
        last_p[...] = spread[...].reshape(chips, 16, 128).astype(BF16)
        last_in[req] = last_p[req]
        each_chip(lambda q: to_chip(last_p.at[q], last_in.at[req], q, 2))

    got(w_on)
    w_sib += go([remote(shard(zo, core), shard(zo, core), sibling)])

    last_c = remote(last_b.at[req], last_b.at[req], sibling)

    @pl.when(core == 1)
    def _():
        all_but_one(last_in, chips - 1, 2).wait_recv()
        tile = last_res[...] + jnp.sum(last_in[...].astype(F32), axis=0)
        power = jnp.sum(jnp.sum(tile * tile, axis=1, keepdims=True), axis=0, keepdims=True)
        last_b[req] = (tile * lax.rsqrt(power / D + EPS) * final_gain[...]).astype(BF16)
        last_c.start()
        last_c.wait_send()

    @pl.when(core == 0)
    def _():
        last_c.wait_recv()

    each_chip(lambda q: to_chip(last_b.at[req], last_b.at[req], q, 4))

    got(w_sib[1:])

    def feed(s):
        xa = rows[s].reshape(SIDE * SIDE * PART, D)
        gu = nt_dot(xa[:, : D // 2], wf[0, 0:2].reshape(2 * PLANE_UNITS, D // 2))
        gu += nt_dot(xa[:, D // 2 :], wf[1, 0:2].reshape(2 * PLANE_UNITS, D // 2))
        gate, up = gu[:, :PLANE_UNITS], gu[:, PLANE_UNITS:]
        active = (gate / (1.0 + jnp.exp(-gate)) * up).astype(BF16)
        for j in range(4):
            down = nn_dot(active, wf[j // 2, 2, :, (j % 2) * 512 : (j % 2 + 1) * 512])
            part[s, :, :, :, j * 512 : (j + 1) * 512] = down.astype(BF16).reshape(
                SIDE, SIDE, PART, 512
            )

    back = [{}, {}]
    near = (2, 1, 3, 0)
    for s in range(2):
        for k in (0, 1, 3, 2):
            got([two[s][k][d] for d in (1, 3, 2)])
        feed(s)
        for k in near:
            i = (inner_at[s] + k) % SIDE
            back[s][k] = go([
                remote(
                    part.at[s, (outer_at[s] + d) % SIDE, i], in1.at[s, d - 1, k],
                    along[outer[s]](d),
                )
                for d in hops
            ])

    all_but_one(last_b, chips - 1, 4).wait_recv()
    unpack(last_b)
    load_voc.wait()
    pick = (
        order[...] == lax.broadcasted_iota(jnp.int32, (ROWS, ROWS), 0)
    ).astype(BF16)
    final_rows = nn_dot(pick, last_x[...]).astype(BF16)
    top = None
    for start in range(0, VOC, VOC_BLOCK):
        stop = min(start + VOC_BLOCK, VOC)
        block = nt_dot(final_rows, voc[start:stop])
        logp[:, start:stop] = block
        m = jnp.max(block, axis=1, keepdims=True)
        top = m if top is None else jnp.maximum(top, m)
    total = jnp.sum(jnp.exp(logp[...] - top), axis=1, keepdims=True)
    eye = lax.broadcasted_iota(jnp.int32, (ROWS, ROWS), 0) == lax.broadcasted_iota(
        jnp.int32, (ROWS, ROWS), 1
    )

    def as_row(col):
        return jnp.sum(jnp.where(eye, col, 0.0), axis=0, keepdims=True)

    me = req * 2 + core
    stats[me] = jnp.concatenate([as_row(top), as_row(total)], axis=1)

    def tell(d, carry):
        q = lax.rem(me + d, 2 * chips)
        pltpu.make_async_remote_copy(
            src_ref=stats.at[me], dst_ref=stats.at[me], send_sem=gsem.at[6], recv_sem=gsem.at[7],
            device_id=(q // 2, q % 2), device_id_type=MESH,
        ).start()
        return carry

    lax.fori_loop(1, 2 * chips, tell, 0)

    ends = [{}, {}]
    keep = [None, None]
    for k in near:
        for s in range(2):
            got(back[s][k])
            i = (inner_at[s] + k) % SIDE
            tot = part[s, outer_at[s], i].astype(F32)
            for d in range(3):
                tot += in1[s, d, k].astype(F32)
            if k == 0:
                keep[s] = tot
            else:
                mid[s, k - 1] = tot.astype(BF16)
                ends[s][k] = go([remote(mid.at[s, k - 1], in2.at[s, k - 1], along[inner[s]](k))])[0]
    for s in range(2):
        span = slice(s * PART, (s + 1) * PART)
        resid[span] = resid[span] + keep[s]

    all_but_one(stats, 2 * chips - 1, 6).wait_recv()
    tops = stats[:, 0, :ROWS]
    m = jnp.max(tops, axis=0, keepdims=True)
    t = jnp.sum(stats[:, 0, ROWS:] * jnp.exp(tops - m), axis=0, keepdims=True)
    top = jnp.sum(jnp.where(eye, m, 0.0), axis=1, keepdims=True)
    log_total = jnp.sum(jnp.where(eye, jnp.log(t), 0.0), axis=1, keepdims=True)
    logp[...] = logp[...] - top - log_total

    for s in range(2):
        got([ends[s][k] for k in (2, 1, 3)])
        span = slice(s * PART, (s + 1) * PART)
        tot = resid[span]
        for d in range(3):
            tot += in2[s, d].astype(F32)
        resid[span] = tot
    stay = pl.ds(pl.multiple_of(core * (D // 2), D // 2), D // 2)
    give = pl.ds(pl.multiple_of(other * (D // 2), D // 2), D // 2)
    out_s[...] = resid[:, give].astype(BF16)
    out_x = go([remote(out_s, out_r, sibling)])
    out[mine] = resid[:, stay].astype(BF16)

    @pl.when(core == 1)
    def _():
        all_but_one(last_a, chips - 1, 0).wait_send()
        all_but_one(last_p, chips - 1, 2).wait_send()

    all_but_one(last_b, chips - 1, 4).wait_send()
    all_but_one(stats, 2 * chips - 1, 6).wait_send()
    for c in sent[:-1]:
        c.wait_send()
    got(out_x)
    out[theirs] = out_r[...]
    out_x[0].wait_send()


def copy_kernel(a, b, a_out, b_out, sem):
    copies = [
        pltpu.make_async_copy(a, a_out, sem.at[0]),
        pltpu.make_async_copy(b, b_out, sem.at[1]),
    ]
    for c in copies:
        c.start()
    for c in copies:
        c.wait()


def on_device(
    hidden_in, attn_gain, w_query, w_key, w_value, query_gain, key_gain, w_out,
    cache_keys, cache_values, cache_lengths, slot_request, mlp_gain, w_gate, w_up, w_down,
    final_gain, w_vocab,
):
    half_dim = HEAD_DIM // 2
    one = ROPE_BASE ** (-2.0 * np.arange(half_dim) / HEAD_DIM)
    freq = jnp.asarray(np.concatenate([one, one])[None].astype(np.float32))
    vmem = pl.BlockSpec(memory_space=pltpu.VMEM)
    smem = pl.BlockSpec(memory_space=pltpu.SMEM)
    far = pl.BlockSpec(memory_space=pl.ANY)
    V = pltpu.VMEM
    S = SIDE
    results = (
        jax.ShapeDtypeStruct((ROWS, D // 2), BF16),
        jax.ShapeDtypeStruct((ROWS, VOC), F32),
    )
    out, logp = pl.pallas_call(
        step_kernel,
        out_shape=results,
        in_specs=[vmem] * 8 + [smem] * 2 + [far] * 10,
        out_specs=(vmem, vmem),
        scratch_shapes=[
            V((ROWS, D), BF16),
            V((D, 1024), BF16), V((D, 512), BF16), V((D, 512), BF16), V((1024, D), BF16),
            V((KEYS, 512), BF16), V((KEYS, 512), BF16), V((VOC, D), BF16),
            V((2, 3, PLANE_UNITS, D // 2), BF16),
            V((4, 2 * ROWS, HEAD_DIM), BF16), V((4, ROWS, HEAD_DIM), BF16), V((ROWS, 512), BF16),
            V((ROWS, 1024), BF16), V((ROWS, D), F32), V((HALF, D), F32), V((16, 128), F32),
            V((HALF, D), F32),
            V((2, S, S, PART, D), BF16), V((2, S, S, PART, D), BF16),
            V((2, 3, S, PART, D), BF16), V((2, 3, PART, D), BF16), V((2, 3, PART, D), BF16),
            V((HALF, D // 2), BF16), V((HALF, D // 2), BF16),
            V((S**3, 16, 128), BF16), V((S**3, 16, 128), BF16), V((S**3, 16, 128), BF16),
            V((S**3, 16, 128), BF16), V((16, 128), F32), V((S**3 * 16, 128), F32),
            V((S**3, D), BF16), V((2 * S**3, 1, 128), F32),
            pltpu.SemaphoreType.DMA((16,)),
            pltpu.SemaphoreType.DMA((N_COPIES,)),
            pltpu.SemaphoreType.DMA((N_COPIES,)),
            pltpu.SemaphoreType.DMA((8,)),
            pltpu.SemaphoreType.REGULAR,
            pltpu.SemaphoreType.REGULAR,
        ],
        compiler_params=pltpu.CompilerParams(
            collective_id=0, has_side_effects=True, vmem_limit_bytes=58 * 1024 * 1024
        ),
    )(
        hidden_in, attn_gain.reshape(1, D), query_gain.reshape(1, HEAD_DIM),
        key_gain.reshape(1, HEAD_DIM), mlp_gain.reshape(8, 128), final_gain.reshape(16, 128), freq,
        slot_request.reshape(1, ROWS), slot_request, cache_lengths,
        w_query, w_key, w_value, w_out, cache_keys, cache_values,
        w_gate.T, w_up.T, w_down, w_vocab.T,
    )
    return pl.pallas_call(
        copy_kernel,
        out_shape=results,
        in_specs=[far] * 2,
        out_specs=(far, far),
        scratch_shapes=[pltpu.SemaphoreType.DMA((2,))],
    )(out, logp)


def solution(mesh):
    in_specs = (
        P("req", None), P(), P(None, "head"), P(None, "head"), P(None, "head"), P(), P(),
        P("head", None), P("req", None, "head"), P("req", None, "head"), P(), P(), P("head"),
        P("head", "req"), P("head", "req"), P("req", "head"), P(), P(None, ("req", "head")),
    )
    out_specs = (P("req", "head"), P(None, ("req", "head")))
    return jax.shard_map(
        on_device, mesh=mesh, in_specs=in_specs, out_specs=out_specs, check_vma=False
    )
```

time: 95.7 us -> 81.3 us (0.85)
  Pallas kernels: 90.8 us -> 80.5 us
  local copies, waits for them, and re-layouts: 3.29 us -> 0 us
    pallas_call x1 -> x2, Pallas kernels: 90.8 us -> 80.5 us  [the longest x1 65.5 us: on_device(): pl.pallas_call(step_kernel, out_shape=results, in_specs=[vmem] * 8 + [sme...]
    unnamed x2 -> x0, local copies, waits for them, and re-layouts: 3.29 us -> none
where the time goes in v2:
time: 81.3 us; the launch traced here: 81.2 us
  Pallas kernels  80.5 us (99%)
    pallas_call x1, Pallas kernels, on_device(): pl.pallas_call(step_kernel, out_shape=results, in_specs=[vmem] * 8 + [sme...  65.5 us
    pallas_call x1, Pallas kernels, on_device(): pl.pallas_call(copy_kernel, out_shape=results, in_specs=[far] * 2, out_sp...  15 us

profile of v2, /device:TPU:1, one launch (start us, length us, event | category | flops | bytes accessed | tf_op | source)
XLA Modules:
  0.0 81.2 jit_solution(9212256530703303662)
XLA Ops:
  0.6 65.5 %shard_map.194 = (bf16[64,1024]{1,0:T(8,128)(2,1)}, f32[64,1187]{1,0:T(8,128)}) custom-call(bf16[64,2048]{1,0:T(8,128)(2,1)} %hidden.1, f32[1,2048]{1,0:T(1,128)} %bitcast.12, f32[1,128]{1,0:T(1,128)} %bitcast.16, f32[1,128]{1,0:T(1,128)} %bitcast.17, f32[8,128]{1,0:T(8,128)} %bitcast.14, f32[16,128]{1,0:T(8,128)} %bitcast.13, f32[1,128]{1,0:T(1,128)} %constant.2.clone.freq, ...), custom_call_target="tpu_custom_call" | custom-call | tf_op jit(solution)/shard_map/pallas_call | solution.py:472
  66.2 15.0 %shard_map.195 = (bf16[64,1024]{1,0:T(8,128)(2,1)}, f32[64,1187]{1,0:T(8,128)}) custom-call(bf16[64,1024]{1,0:T(8,128)(2,1)} %get-tuple-element.4.a, f32[64,1187]{1,0:T(8,128)} %get-tuple-element.5.b), custom_call_target="tpu_custom_call" | custom-call | tf_op jit(solution)/shard_map/pallas_call | solution.py:508

commit v3 on v2

--- a/solution.py
+++ b/solution.py
@@ -26,7 +26,7 @@
 UNITS = 96
 PLANE_UNITS = SIDE * UNITS
 KEYS = 2048
-KEY_BLOCK = 512
+KEY_BLOCK = 1024
 VOC = 1187
 VOC_BLOCK = 256
 N_COPIES = 100
@@ -43,8 +43,8 @@
 def step_kernel(
     hidden, attn_gain, query_gain, key_gain, mlp_gain, final_gain, freq, order, order_s, lengths,
     w_query, w_key, w_value, w_out, cache_k, cache_v, w_gate, w_up, w_down, w_vocab,
-    out, logp,
-    normed, wq, wk, wv, wo, kc, vc, voc, wf, qs, kn, vn, att, proj, proj_in, gains, resid,
+    out_hbm, logp_hbm,
+    out, logp, normed, wq, wk, wv, wo, kc, vc, voc, wf, qs, kn, vn, att, proj, proj_in, gains, resid,
     rows, part, in1, mid, in2, out_s, out_r,
     last_a, last_p, last_in, last_b, last_res, spread, last_x, stats,
     lsem, ssem, rsem, gsem, plane_sem, all_sem,
@@ -92,21 +92,32 @@
         for c in copies:
             c.wait_recv()
 
-    load_k = local(w_key, wk)
-    load_v = local(w_value, wv)
-    load_q = local(w_query, wq)
-    load_kc = local(cache_k.at[0], kc)
-    load_vc = local(cache_v.at[0], vc)
-    load_o = local(w_out, wo)
-    load_voc = local(w_vocab, voc)
+    def load(src, dst, parts):
+        n = src.shape[0] // parts
+        return [local(src.at[pl.ds(k * n, n)], dst.at[pl.ds(k * n, n)]) for k in range(parts)]
+
+    def begin(copies):
+        for c in copies:
+            c.start()
+
+    def done_with(copies):
+        for c in copies:
+            c.wait()
+
+    load_k = load(w_key, wk, 2)
+    load_v = load(w_value, wv, 2)
+    load_q = load(w_query, wq, 4)
+    load_kc = load(cache_k.at[0], kc, 2)
+    load_vc = load(cache_v.at[0], vc, 2)
+    load_o = load(w_out, wo, 4)
+    load_voc = [local(w_vocab, voc)]
     unit_at = pl.multiple_of(z * UNITS, UNITS)
     load_own = [
         local(w, wf.at[core, k, pl.ds(unit_at, UNITS)]) for k, w in enumerate((w_gate, w_up, w_down))
     ]
     my_gain = gains.at[pl.ds(pl.multiple_of(core * 8, 8), 8)]
     load_gain = local(mlp_gain, my_gain)
-    for c in [load_k, load_v, load_q] + load_own + [load_gain, load_kc, load_vc, load_o]:
-        c.start()
+    begin(load_own + [load_gain] + load_k + load_v + load_q + load_kc + load_vc + load_o)
 
     barrier = pltpu.get_barrier_semaphore()
     peers = [sibling]
@@ -115,32 +126,6 @@
     for p in peers:
         pl.semaphore_signal(barrier, inc=1, device_id=p, device_id_type=MESH)
 
-    tokens = hidden[...].astype(F32)
-    scale = lax.rsqrt(jnp.mean(tokens * tokens, axis=-1, keepdims=True) + EPS)
-    normed[...] = (tokens * scale * attn_gain[...]).astype(BF16)
-    slot = order_s[req]
-    length = lengths[slot]
-    position = (length + lax.broadcasted_iota(jnp.int32, (ROWS, 1), 0)).astype(F32)
-    angle = position * freq[...]
-    cosine = jnp.cos(angle)
-    lane = lax.broadcasted_iota(jnp.int32, (ROWS, HEAD_DIM), 1)
-    sine = jnp.where(lane < HEAD_DIM // 2, -jnp.sin(angle), jnp.sin(angle))
-
-    def rotated(v, gain):
-        v = v * lax.rsqrt(jnp.mean(v * v, axis=-1, keepdims=True) + EPS) * gain
-        return (v * cosine + pltpu.roll(v, HEAD_DIM // 2, 1) * sine).astype(BF16)
-
-    load_k.wait()
-    for j in range(2):
-        both = nn_dot(normed[...], wk[:, j * 256 : (j + 1) * 256])
-        for i in range(2):
-            kn[2 * j + i] = rotated(both[:, i * 128 : (i + 1) * 128], key_gain[...])
-    load_v.wait()
-    for j in range(2):
-        vn[:, j * 256 : (j + 1) * 256] = nn_dot(
-            normed[...], wv[:, j * 256 : (j + 1) * 256]
-        ).astype(BF16)
-
     def shard(zz, h):
         return wf.at[h, :, pl.ds(pl.multiple_of(zz * UNITS, UNITS), UNITS)]
 
@@ -149,8 +134,7 @@
         return wf.at[h, :, pl.ds(pl.multiple_of(zz * UNITS + k * n, n), n)]
 
     zm, zp, zo = (z + 3) % SIDE, (z + 1) % SIDE, (z + 2) % SIDE
-    for c in load_own + [load_gain]:
-        c.wait()
+    done_with(load_own + [load_gain])
     pl.semaphore_wait(barrier, len(peers))
     w_first, w_second = [], []
     for copies, k_up in ((w_first, 0), (w_second, 1)):
@@ -163,7 +147,33 @@
     for d in (1, 2, 3):
         pl.semaphore_signal(plane_sem, inc=1, device_id=along["y"](d), device_id_type=MESH)
 
-    load_q.wait()
+    tokens = hidden[...].astype(F32)
+    scale = lax.rsqrt(jnp.mean(tokens * tokens, axis=-1, keepdims=True) + EPS)
+    normed[...] = (tokens * scale * attn_gain[...]).astype(BF16)
+    slot = order_s[req]
+    length = lengths[slot]
+    position = (length + lax.broadcasted_iota(jnp.int32, (ROWS, 1), 0)).astype(F32)
+    angle = position * freq[...]
+    cosine = jnp.cos(angle)
+    lane = lax.broadcasted_iota(jnp.int32, (ROWS, HEAD_DIM), 1)
+    sine = jnp.where(lane < HEAD_DIM // 2, -jnp.sin(angle), jnp.sin(angle))
+
+    def rotated(v, gain):
+        v = v * lax.rsqrt(jnp.mean(v * v, axis=-1, keepdims=True) + EPS) * gain
+        return (v * cosine + pltpu.roll(v, HEAD_DIM // 2, 1) * sine).astype(BF16)
+
+    done_with(load_k)
+    for j in range(2):
+        both = nn_dot(normed[...], wk[:, j * 256 : (j + 1) * 256])
+        for i in range(2):
+            kn[2 * j + i] = rotated(both[:, i * 128 : (i + 1) * 128], key_gain[...])
+    done_with(load_v)
+    for j in range(2):
+        vn[:, j * 256 : (j + 1) * 256] = nn_dot(
+            normed[...], wv[:, j * 256 : (j + 1) * 256]
+        ).astype(BF16)
+
+    done_with(load_q)
     for j in range(4):
         both = nn_dot(normed[...], wq[:, j * 256 : (j + 1) * 256])
         for i in range(2):
@@ -171,9 +181,9 @@
                 both[:, i * 128 : (i + 1) * 128], query_gain[...]
             )
 
-    load_kc.wait()
-    load_vc.wait()
-    load_voc.start()
+    done_with(load_kc)
+    done_with(load_vc)
+    begin(load_voc)
     slope = LOG2E / math.sqrt(HEAD_DIM)
     base = SHIFT * LOG2E
     row_at = lax.broadcasted_iota(jnp.int32, (2 * ROWS, ROWS), 0) % ROWS
@@ -199,7 +209,7 @@
     for g in range(4):
         one_head(g)
 
-    load_o.wait()
+    done_with(load_o)
     for j in range(4):
         cols = slice(j * 512, (j + 1) * 512)
         proj[:, cols] = nn_dot(att[...], wo[:, cols])
@@ -221,7 +231,7 @@
 
     inner, outer = ("x", "y"), ("y", "x")
     inner_at, outer_at = (x, y), (y, x)
-    hops = (2, 1, 3)
+    hops = (1, 3, 2)
 
     def piece(s, o, i):
         return rows.at[s, o % SIDE, i % SIDE]
@@ -229,9 +239,6 @@
     def push(s, i, axis):
         b = piece(s, outer_at[s], i)
         return {d: go([remote(b, b, along[axis](d))])[0] for d in hops}
-
-    one = [push(s, inner_at[s], inner[s]) for s in range(2)]
-    two = [{0: push(s, inner_at[s], outer[s])} for s in range(2)]
 
     def each_chip(body):
         def step(d, carry):
@@ -265,19 +272,13 @@
         last_a[req] = (tile * lax.rsqrt(power / D + EPS) * gains[...]).astype(BF16)
         each_chip(lambda q: to_chip(last_a.at[req], last_a.at[req], q, 0))
 
+    one = [push(s, inner_at[s], inner[s]) for s in range(2)]
+    two = [{0: push(s, inner_at[s], outer[s])} for s in range(2)]
     got(w_first)
     w_on = go([
         remote(half_shard(zm, core, 0), half_shard(zm, core, 0), along["z"](1)),
         remote(half_shard(zp, core, 1), half_shard(zp, core, 1), along["z"](-1)),
     ])
-
-    for d in (1, 3, 2):
-        for s in range(2):
-            one[s][d].wait_recv()
-            two[s][d] = push(s, inner_at[s] - d + SIDE, outer[s])
-    got(w_second)
-    w_sib += go([remote(shard(zm, core), shard(zm, core), sibling)])
-    w_sib += go([remote(shard(zp, core), shard(zp, core), sibling)])
 
     def unpack(tiles):
         spread[...] = tiles[...].astype(F32).reshape(chips * 16, 128)
@@ -303,10 +304,21 @@
         last_in[req] = last_p[req]
         each_chip(lambda q: to_chip(last_p.at[q], last_in.at[req], q, 2))
 
+    for d in (1, 3, 2):
+        for s in range(2):
+            one[s][d].wait_recv()
+            two[s][d] = push(s, inner_at[s] - d + SIDE, outer[s])
+
+    got(w_second)
+    w_sib += go([remote(shard(zm, core), shard(zm, core), sibling)])
+    w_sib += go([remote(shard(zp, core), shard(zp, core), sibling)])
     got(w_on)
     w_sib += go([remote(shard(zo, core), shard(zo, core), sibling)])
 
     last_c = remote(last_b.at[req], last_b.at[req], sibling)
+
+    def tell_final():
+        each_chip(lambda q: to_chip(last_b.at[req], last_b.at[req], q, 4))
 
     @pl.when(core == 1)
     def _():
@@ -315,47 +327,61 @@
         power = jnp.sum(jnp.sum(tile * tile, axis=1, keepdims=True), axis=0, keepdims=True)
         last_b[req] = (tile * lax.rsqrt(power / D + EPS) * final_gain[...]).astype(BF16)
         last_c.start()
+        tell_final()
         last_c.wait_send()
 
-    @pl.when(core == 0)
-    def _():
-        last_c.wait_recv()
-
-    each_chip(lambda q: to_chip(last_b.at[req], last_b.at[req], q, 4))
-
     got(w_sib[1:])
-
-    def feed(s):
-        xa = rows[s].reshape(SIDE * SIDE * PART, D)
+    block_rows = SIDE * PART
+
+    def feed(k):
+        own = [(outer_at[s] + k) % SIDE for s in range(2)]
+        xa = jnp.concatenate([rows[s, own[s]].reshape(block_rows, D) for s in range(2)], axis=0)
         gu = nt_dot(xa[:, : D // 2], wf[0, 0:2].reshape(2 * PLANE_UNITS, D // 2))
         gu += nt_dot(xa[:, D // 2 :], wf[1, 0:2].reshape(2 * PLANE_UNITS, D // 2))
         gate, up = gu[:, :PLANE_UNITS], gu[:, PLANE_UNITS:]
         active = (gate / (1.0 + jnp.exp(-gate)) * up).astype(BF16)
         for j in range(4):
             down = nn_dot(active, wf[j // 2, 2, :, (j % 2) * 512 : (j % 2 + 1) * 512])
-            part[s, :, :, :, j * 512 : (j + 1) * 512] = down.astype(BF16).reshape(
-                SIDE, SIDE, PART, 512
-            )
+            down = down.astype(BF16).reshape(2, SIDE, PART, 512)
+            for s in range(2):
+                part[s, own[s], :, :, j * 512 : (j + 1) * 512] = down[s]
 
     back = [{}, {}]
     near = (2, 1, 3, 0)
-    for s in range(2):
-        for k in (0, 1, 3, 2):
-            got([two[s][k][d] for d in (1, 3, 2)])
-        feed(s)
-        for k in near:
-            i = (inner_at[s] + k) % SIDE
-            back[s][k] = go([
-                remote(
-                    part.at[s, (outer_at[s] + d) % SIDE, i], in1.at[s, d - 1, k],
-                    along[outer[s]](d),
-                )
-                for d in hops
-            ])
+
+    def give_back(k):
+        for i in near:
+            for s in range(2):
+                ii = (inner_at[s] + i) % SIDE
+                back[s][k, i] = go([
+                    remote(
+                        part.at[s, (outer_at[s] + k) % SIDE, ii], in1.at[s, k - 1, i],
+                        along[outer[s]](k),
+                    )
+                ])[0]
+
+    def arrived(d):
+        got([two[s][k][d] for k in (0, 1, 3, 2) for s in range(2)])
+
+    feed(0)
+
+    @pl.when(core == 0)
+    def _():
+        last_c.wait_recv()
+        tell_final()
+
+    arrived(1)
+    feed(3)
+    give_back(3)
+    arrived(3)
+    feed(1)
+    give_back(1)
+    arrived(2)
+    feed(2)
 
     all_but_one(last_b, chips - 1, 4).wait_recv()
     unpack(last_b)
-    load_voc.wait()
+    done_with(load_voc)
     pick = (
         order[...] == lax.broadcasted_iota(jnp.int32, (ROWS, ROWS), 0)
     ).astype(BF16)
@@ -387,12 +413,13 @@
         return carry
 
     lax.fori_loop(1, 2 * chips, tell, 0)
+    give_back(2)
 
     ends = [{}, {}]
     keep = [None, None]
     for k in near:
         for s in range(2):
-            got(back[s][k])
+            got([back[s][o, k] for o in (3, 1, 2)])
             i = (inner_at[s] + k) % SIDE
             tot = part[s, outer_at[s], i].astype(F32)
             for d in range(3):
@@ -413,6 +440,8 @@
     top = jnp.sum(jnp.where(eye, m, 0.0), axis=1, keepdims=True)
     log_total = jnp.sum(jnp.where(eye, jnp.log(t), 0.0), axis=1, keepdims=True)
     logp[...] = logp[...] - top - log_total
+    save_logp = local(logp, logp_hbm)
+    save_logp.start()
 
     for s in range(2):
         got([ends[s][k] for k in (2, 1, 3)])
@@ -438,18 +467,11 @@
         c.wait_send()
     got(out_x)
     out[theirs] = out_r[...]
+    save_out = local(out, out_hbm)
+    save_out.start()
     out_x[0].wait_send()
-
-
-def copy_kernel(a, b, a_out, b_out, sem):
-    copies = [
-        pltpu.make_async_copy(a, a_out, sem.at[0]),
-        pltpu.make_async_copy(b, b_out, sem.at[1]),
-    ]
-    for c in copies:
-        c.start()
-    for c in copies:
-        c.wait()
+    save_logp.wait()
+    save_out.wait()
 
 
 def on_device(
@@ -473,8 +495,9 @@
         step_kernel,
         out_shape=results,
         in_specs=[vmem] * 8 + [smem] * 2 + [far] * 10,
-        out_specs=(vmem, vmem),
+        out_specs=(far, far),
         scratch_shapes=[
+            V((ROWS, D // 2), BF16), V((ROWS, VOC), F32),
             V((ROWS, D), BF16),
             V((D, 1024), BF16), V((D, 512), BF16), V((D, 512), BF16), V((1024, D), BF16),
             V((KEYS, 512), BF16), V((KEYS, 512), BF16), V((VOC, D), BF16),
@@ -488,7 +511,7 @@
             V((S**3, 16, 128), BF16), V((S**3, 16, 128), BF16), V((S**3, 16, 128), BF16),
             V((S**3, 16, 128), BF16), V((16, 128), F32), V((S**3 * 16, 128), F32),
             V((S**3, D), BF16), V((2 * S**3, 1, 128), F32),
-            pltpu.SemaphoreType.DMA((16,)),
+            pltpu.SemaphoreType.DMA((32,)),
             pltpu.SemaphoreType.DMA((N_COPIES,)),
             pltpu.SemaphoreType.DMA((N_COPIES,)),
             pltpu.SemaphoreType.DMA((8,)),
@@ -505,13 +528,7 @@
         w_query, w_key, w_value, w_out, cache_keys, cache_values,
         w_gate.T, w_up.T, w_down, w_vocab.T,
     )
-    return pl.pallas_call(
-        copy_kernel,
-        out_shape=results,
-        in_specs=[far] * 2,
-        out_specs=(far, far),
-        scratch_shapes=[pltpu.SemaphoreType.DMA((2,))],
-    )(out, logp)
+    return out, logp
 
 
 def solution(mesh):

time: 81.3 us -> 67.6 us (0.83)
  Pallas kernels: 80.5 us -> 63.5 us
  local copies, waits for them, and re-layouts: 0 us -> 3.29 us
    pallas_call x1 -> x0, Pallas kernels: 15 us -> none  [on_device(): pl.pallas_call(copy_kernel, out_shape=results, in_specs=[far] * 2, out_sp...]
    unnamed x0 -> x2, local copies, waits for them, and re-layouts: none -> 3.29 us
    pallas_call x1, Pallas kernels: 65.5 us -> 63.5 us  [on_device(): pl.pallas_call(step_kernel, out_shape=results, in_specs=[vmem] * 8 + [sme...]
where the time goes in v3:
time: 67.6 us; the launch traced here: 67.4 us
  Pallas kernels  63.5 us (94%)
  local copies, waits for them, and re-layouts  3.29 us (5%)
    pallas_call x1, Pallas kernels, on_device(): pl.pallas_call(step_kernel, out_shape=results, in_specs=[vmem] * 8 + [sme...  63.5 us
    unnamed x2, local copies, waits for them, and re-layouts  3.29 us

profile of v3, /device:TPU:1, one launch (start us, length us, event | category | flops | bytes accessed | tf_op | source)
XLA Modules:
  0.0 67.4 jit_solution(14076624837976856230)
XLA Ops:
  0.6 63.5 %shard_map.194 = (bf16[64,1024]{1,0:T(8,128)(2,1)}, f32[64,1187]{1,0:T(8,128)}) custom-call(bf16[64,2048]{1,0:T(8,128)(2,1)} %hidden.1, f32[1,2048]{1,0:T(1,128)} %bitcast.12, f32[1,128]{1,0:T(1,128)} %bitcast.16, f32[1,128]{1,0:T(1,128)} %bitcast.17, f32[8,128]{1,0:T(8,128)} %bitcast.14, f32[16,128]{1,0:T(8,128)} %bitcast.13, f32[1,128]{1,0:T(1,128)} %constant.2.clone.freq, ...), custom_call_target="tpu_custom_call" | custom-call | tf_op jit(solution)/shard_map/pallas_call | solution.py:494
  64.2 1.6 %copy.23 = bf16[64,1024]{1,0:T(8,128)(2,1)} copy(bf16[64,1024]{1,0:T(8,128)(2,1)} %get-tuple-element.4) | data formatting | bytes 262144
  65.7 1.7 %copy.24 = f32[64,1187]{1,0:T(8,128)} copy(f32[64,1187]{1,0:T(8,128)} %get-tuple-element.5) | data formatting | bytes 607744

commit v4 on v3

--- a/solution.py
+++ b/solution.py
@@ -363,21 +363,22 @@
     def arrived(d):
         got([two[s][k][d] for k in (0, 1, 3, 2) for s in range(2)])
 
-    feed(0)
+    arrived(1)
+    feed(3)
 
     @pl.when(core == 0)
     def _():
         last_c.wait_recv()
         tell_final()
 
-    arrived(1)
-    feed(3)
     give_back(3)
     arrived(3)
     feed(1)
     give_back(1)
     arrived(2)
     feed(2)
+    give_back(2)
+    feed(0)
 
     all_but_one(last_b, chips - 1, 4).wait_recv()
     unpack(last_b)
@@ -413,7 +414,6 @@
         return carry
 
     lax.fori_loop(1, 2 * chips, tell, 0)
-    give_back(2)
 
     ends = [{}, {}]
     keep = [None, None]
@@ -472,6 +472,11 @@
     out_x[0].wait_send()
     save_logp.wait()
     save_out.wait()
+
+
+def copy_kernel(a, b, a_out, b_out):
+    a_out[...] = a[...]
+    b_out[...] = b[...]
 
 
 def on_device(
@@ -528,7 +533,12 @@
         w_query, w_key, w_value, w_out, cache_keys, cache_values,
         w_gate.T, w_up.T, w_down, w_vocab.T,
     )
-    return out, logp
+    return pl.pallas_call(
+        copy_kernel,
+        out_shape=results,
+        in_specs=[vmem] * 2,
+        out_specs=(vmem, vmem),
+    )(out, logp)
 
 
 def solution(mesh):

time: 67.6 us -> 63.7 us (0.942)
  local copies, waits for them, and re-layouts: 3.29 us -> 0 us
    unnamed x2 -> x0, local copies, waits for them, and re-layouts: 3.29 us -> none
    pallas_call x1, Pallas kernels: 63.5 us -> 61.1 us  [on_device(): pl.pallas_call(step_kernel, out_shape=results, in_specs=[vmem] * 8 + [sme...]
    pallas_call x0 -> x1, Pallas kernels: none -> 1.82 us  [on_device(): pl.pallas_call(copy_kernel, out_shape=results, in_specs=[vmem] * 2, out_s...]
where the time goes in v4:
time: 63.7 us; the launch traced here: 63.6 us
  Pallas kernels  62.9 us (99%)
  between operations  0.65 us (1%)
    pallas_call x1, Pallas kernels, on_device(): pl.pallas_call(step_kernel, out_shape=results, in_specs=[vmem] * 8 + [sme...  61.1 us
    pallas_call x1, Pallas kernels, on_device(): pl.pallas_call(copy_kernel, out_shape=results, in_specs=[vmem] * 2, out_s...  1.82 us

profile of v4, /device:TPU:1, one launch (start us, length us, event | category | flops | bytes accessed | tf_op | source)
XLA Modules:
  0.0 63.6 jit_solution(3543536315911570108)
XLA Ops:
  0.6 61.1 %shard_map.194 = (bf16[64,1024]{1,0:T(8,128)(2,1)}, f32[64,1187]{1,0:T(8,128)}) custom-call(bf16[64,2048]{1,0:T(8,128)(2,1)} %hidden.1, f32[1,2048]{1,0:T(1,128)} %bitcast.12, f32[1,128]{1,0:T(1,128)} %bitcast.16, f32[1,128]{1,0:T(1,128)} %bitcast.17, f32[8,128]{1,0:T(8,128)} %bitcast.14, f32[16,128]{1,0:T(8,128)} %bitcast.13, f32[1,128]{1,0:T(1,128)} %constant.2.clone.freq, ...), custom_call_target="tpu_custom_call" | custom-call | tf_op jit(solution)/shard_map/pallas_call | solution.py:499
  61.7 1.8 %shard_map.195 = (bf16[64,1024]{1,0:T(8,128)(2,1)}, f32[64,1187]{1,0:T(8,128)}) custom-call(bf16[64,1024]{1,0:T(8,128)(2,1)} %get-tuple-element.4.a, f32[64,1187]{1,0:T(8,128)} %get-tuple-element.5.b), custom_call_target="tpu_custom_call" | custom-call | tf_op jit(solution)/shard_map/pallas_call | solution.py:536

commit v5 on v4

--- a/solution.py
+++ b/solution.py
@@ -210,12 +210,15 @@
         one_head(g)
 
     done_with(load_o)
+    mine = pl.ds(pl.multiple_of(core * HALF, HALF), HALF)
+    theirs = pl.ds(pl.multiple_of(other * HALF, HALF), HALF)
+    proj_x = []
     for j in range(4):
         cols = slice(j * 512, (j + 1) * 512)
         proj[:, cols] = nn_dot(att[...], wo[:, cols])
-    mine = pl.ds(pl.multiple_of(core * HALF, HALF), HALF)
-    theirs = pl.ds(pl.multiple_of(other * HALF, HALF), HALF)
-    proj_x = go([remote(proj.at[theirs], proj_in, sibling)])
+        proj_x += go([
+            remote(proj.at[theirs, pl.ds(j * 512, 512)], proj_in.at[:, pl.ds(j * 512, 512)], sibling)
+        ])
     pl.semaphore_wait(plane_sem, 3)
     for d in (1, 2, 3):
         pl.semaphore_signal(all_sem, inc=1, device_id=along["z"](d), device_id_type=MESH)
@@ -318,7 +321,14 @@
     last_c = remote(last_b.at[req], last_b.at[req], sibling)
 
     def tell_final():
-        each_chip(lambda q: to_chip(last_b.at[req], last_b.at[req], q, 4))
+        def both(q):
+            for c in (core, other):
+                pltpu.make_async_remote_copy(
+                    src_ref=last_b.at[req], dst_ref=last_b.at[req], send_sem=gsem.at[4],
+                    recv_sem=gsem.at[5], device_id=(q, c), device_id_type=MESH,
+                ).start()
+
+        each_chip(both)
 
     @pl.when(core == 1)
     def _():
@@ -333,18 +343,18 @@
     got(w_sib[1:])
     block_rows = SIDE * PART
 
-    def feed(k):
-        own = [(outer_at[s] + k) % SIDE for s in range(2)]
-        xa = jnp.concatenate([rows[s, own[s]].reshape(block_rows, D) for s in range(2)], axis=0)
+    def feed(*ks):
+        blocks = [(s, (outer_at[s] + k) % SIDE) for k in ks for s in range(2)]
+        xa = jnp.concatenate([rows[s, o].reshape(block_rows, D) for s, o in blocks], axis=0)
         gu = nt_dot(xa[:, : D // 2], wf[0, 0:2].reshape(2 * PLANE_UNITS, D // 2))
         gu += nt_dot(xa[:, D // 2 :], wf[1, 0:2].reshape(2 * PLANE_UNITS, D // 2))
         gate, up = gu[:, :PLANE_UNITS], gu[:, PLANE_UNITS:]
         active = (gate / (1.0 + jnp.exp(-gate)) * up).astype(BF16)
         for j in range(4):
             down = nn_dot(active, wf[j // 2, 2, :, (j % 2) * 512 : (j % 2 + 1) * 512])
-            down = down.astype(BF16).reshape(2, SIDE, PART, 512)
-            for s in range(2):
-                part[s, own[s], :, :, j * 512 : (j + 1) * 512] = down[s]
+            down = down.astype(BF16).reshape(len(blocks), SIDE, PART, 512)
+            for b, (s, o) in enumerate(blocks):
+                part[s, o, :, :, j * 512 : (j + 1) * 512] = down[b]
 
     back = [{}, {}]
     near = (2, 1, 3, 0)
@@ -364,21 +374,18 @@
         got([two[s][k][d] for k in (0, 1, 3, 2) for s in range(2)])
 
     arrived(1)
-    feed(3)
-
-    @pl.when(core == 0)
-    def _():
-        last_c.wait_recv()
-        tell_final()
-
+    arrived(3)
+    feed(3, 1)
     give_back(3)
-    arrived(3)
-    feed(1)
     give_back(1)
     arrived(2)
     feed(2)
     give_back(2)
     feed(0)
+
+    @pl.when(core == 0)
+    def _():
+        last_c.wait_recv()
 
     all_but_one(last_b, chips - 1, 4).wait_recv()
     unpack(last_b)
@@ -460,8 +467,9 @@
     def _():
         all_but_one(last_a, chips - 1, 0).wait_send()
         all_but_one(last_p, chips - 1, 2).wait_send()
-
-    all_but_one(last_b, chips - 1, 4).wait_send()
+        for _ in range(2):
+            all_but_one(last_b, chips - 1, 4).wait_send()
+
     all_but_one(stats, 2 * chips - 1, 6).wait_send()
     for c in sent[:-1]:
         c.wait_send()

time: 63.7 us -> 61.6 us (0.967)
  Pallas kernels: 62.9 us -> 60.8 us
    pallas_call x1, Pallas kernels: 61.1 us -> 58.9 us  [on_device(): pl.pallas_call(step_kernel, out_shape=results, in_specs=[vmem] * 8 + [sme...]
where the time goes in v5:
time: 61.6 us; the launch traced here: 61.4 us
  Pallas kernels  60.8 us (99%)
  between operations  0.65 us (1%)
    pallas_call x1, Pallas kernels, on_device(): pl.pallas_call(step_kernel, out_shape=results, in_specs=[vmem] * 8 + [sme...  58.9 us
    pallas_call x1, Pallas kernels, on_device(): pl.pallas_call(copy_kernel, out_shape=results, in_specs=[vmem] * 2, out_s...  1.82 us

profile of v5, /device:TPU:1, one launch (start us, length us, event | category | flops | bytes accessed | tf_op | source)
XLA Modules:
  0.0 61.4 jit_solution(17491394465291100581)
XLA Ops:
  0.6 58.9 %shard_map.194 = (bf16[64,1024]{1,0:T(8,128)(2,1)}, f32[64,1187]{1,0:T(8,128)}) custom-call(bf16[64,2048]{1,0:T(8,128)(2,1)} %hidden.1, f32[1,2048]{1,0:T(1,128)} %bitcast.12, f32[1,128]{1,0:T(1,128)} %bitcast.16, f32[1,128]{1,0:T(1,128)} %bitcast.17, f32[8,128]{1,0:T(8,128)} %bitcast.14, f32[16,128]{1,0:T(8,128)} %bitcast.13, f32[1,128]{1,0:T(1,128)} %constant.2.clone.freq, ...), custom_call_target="tpu_custom_call" | custom-call | tf_op jit(solution)/shard_map/pallas_call | solution.py:507
  59.6 1.8 %shard_map.195 = (bf16[64,1024]{1,0:T(8,128)(2,1)}, f32[64,1187]{1,0:T(8,128)}) custom-call(bf16[64,1024]{1,0:T(8,128)(2,1)} %get-tuple-element.4.a, f32[64,1187]{1,0:T(8,128)} %get-tuple-element.5.b), custom_call_target="tpu_custom_call" | custom-call | tf_op jit(solution)/shard_map/pallas_call | solution.py:544
